TPU v7x, 256 devices: a whole 4x4x8 slice. The times are simulated.
256 devices in a mesh: lev: 8 (over z_lo, y), hor: 32 (over z_hi, x, core).
Axes of the slice: x: 4, y: 4, z: 8 (z_hi: 4, z_lo: 2; z = z_hi * 2 + z_lo), core: 2. Of those that a mesh axis runs over, the one named last changes fastest.
Arguments:
- heat_field: float32 [256, 512, 512], P('lev', 'hor'), may hold values from -6 to 6
- saline_field: float32 [256, 512, 512], P('lev', 'hor'), may hold values from -6 to 6
- updraft_speed: float32 [256, 512, 512], P('lev', 'hor'), may hold values from -3 to 3
- heat_mixing_rates: float32 [256], P('lev'), may hold values from 0.05 to 1
- saline_mixing_rates: float32 [256], P('lev'), may hold values from 0.05 to 1
- cross_mixing_rates: float32 [256], P('lev'), may hold values from 0.2 to 1
Outputs:
- updated_heat_field: float32 [256, 512, 512], P('lev', 'hor')
- salt_out: float32 [256, 512, 512], P('lev', 'hor')
All inputs are finite; a program needn't handle non-finite values.
Results may differ from a plain program's by a relative error of at most 0.000073.
Values sent between devices are 32-bit elements; how exact they have to be, the bound alone decides.
No kernel may reach another device: no remote copies, remote signals or barrier semaphores. Data moves between devices by JAX's collectives and lax.ppermute only.
A program may use at most 128 MiB of HBM per device.

v0:
```python
import math

import jax
import jax.numpy as jnp
from jax import lax
from jax.sharding import PartitionSpec as P

highest = lax.Precision.HIGHEST
buoyancy = 0.5
advective_number = 0.25


def extended_2(block, sides, width):
    for axis, dim in sides:
        count = lax.axis_size(axis)
        forward = [(i, i + 1) for i in range(count - 1)]
        backward = [(target, source) for source, target in forward]
        low = lax.ppermute(
            lax.slice_in_dim(block, block.shape[dim] - width, None, axis=dim), axis, forward
        )
        high = lax.ppermute(lax.slice_in_dim(block, 0, width, axis=dim), axis, backward)
        block = jnp.concatenate([low, block, high], axis=dim)
    return block


def wave_angles(left, right, length):
    product = left[:, None] * right[None, :] % length
    return 2.0 * math.pi / length * product.astype(jnp.float32)


def slot_waves(block, within, slot_count, length):
    paired = slot_count // 2
    upper_wave = (length - paired * block - (within - paired)) % length
    waves = jnp.where(within < paired, paired * block + within, upper_wave)
    waves = jnp.where((block == 0) & (within == paired), length // 2, waves)
    return waves


def signed_wave(waves, length):
    return jnp.where(waves < length // 2, waves, waves - length).astype(jnp.float32)


def contract(form, left, right):
    return jnp.einsum(form, left, right, precision=highest)


def complex_product(real_part, imag_part, form, cos_table, sin_table, sign):
    real_out = contract(form, real_part, cos_table) - sign * contract(form, imag_part, sin_table)
    imag_out = contract(form, imag_part, cos_table) + sign * contract(form, real_part, sin_table)
    return (real_out, imag_out)


def multiplied_nonimag_share(field, form, cos_table, sin_table, sign):
    return (contract(form, field, cos_table), sign * contract(form, field, sin_table))


def shards(
    heat_field,
    saline_field,
    updraft_speed,
    heat_mixing_rates,
    saline_mixing_rates,
    cross_mixing_rates,
):
    number_of_layers, number_of_lines, number_of_stacks = heat_field.shape
    parts = lax.axis_size("hor")
    block_index = lax.axis_index("hor")
    length_x = number_of_lines * parts
    slot_count = number_of_stacks // parts
    every_slot = jnp.arange(number_of_stacks)
    all_waves = slot_waves(
        every_slot // slot_count, every_slot % slot_count, slot_count, number_of_stacks
    )
    angle_y = wave_angles(jnp.arange(number_of_stacks), all_waves, number_of_stacks)
    north_cos_lookup = jnp.cos(angle_y).reshape(number_of_stacks, parts, slot_count)
    north_sin_lookup = jnp.sin(angle_y).reshape(number_of_stacks, parts, slot_count)
    x_points = jnp.arange(length_x)
    angle_x = wave_angles(x_points, x_points, length_x)
    cos_x = jnp.cos(angle_x)
    sin_x = jnp.sin(angle_x)
    within = jnp.arange(slot_count)
    wave_y = signed_wave(
        slot_waves(block_index, within, slot_count, number_of_stacks), number_of_stacks
    )
    wave_x = signed_wave(x_points, length_x)
    modulus = (wave_y[:, None] * wave_y[:, None] + wave_x[None, :] * wave_x[None, :]) / (
        length_x / 2.0 * (length_x / 2.0)
    )
    normalizing_factor = 1.0 / (length_x * number_of_stacks)

    def split_into_groups(array):
        return array.reshape(number_of_layers, parts, number_of_lines * slot_count)

    def inverse_x(real_part, imag_part):
        real_out, imag_out = complex_product(real_part, imag_part, "zjm,mx->zxj", cos_x, sin_x, 1.0)
        return (split_into_groups(real_out), split_into_groups(imag_out))

    heat_north_inphase, heat_north_quadrature = multiplied_nonimag_share(
        heat_field, "uhq,qvj->uvhj", north_cos_lookup, north_sin_lookup, -1.0
    )
    salt_y_real, salt_y_imag = multiplied_nonimag_share(
        saline_field, "uhq,qvj->uvhj", north_cos_lookup, north_sin_lookup, -1.0
    )
    pieces = (
        lax.all_to_all(
            split_into_groups(heat_north_inphase), "hor", split_axis=1, concat_axis=1, tiled=True
        ),
        lax.all_to_all(
            split_into_groups(heat_north_quadrature), "hor", split_axis=1, concat_axis=1, tiled=True
        ),
        lax.all_to_all(
            split_into_groups(salt_y_real), "hor", split_axis=1, concat_axis=1, tiled=True
        ),
        lax.all_to_all(
            split_into_groups(salt_y_imag), "hor", split_axis=1, concat_axis=1, tiled=True
        ),
    )
    count = pieces[0].shape[0]
    shaped = [piece.reshape(count, length_x, slot_count) for piece in pieces]
    results = []
    for start in range(0, len(shaped), 2):
        results.extend(
            complex_product(shaped[start], shaped[start + 1], "zxj,xm->zjm", cos_x, sin_x, -1.0)
        )
    heat_nonimag_share, temp_imag, salt_real, salt_imag = tuple(results)
    diag_temp = 1.0 + heat_mixing_rates[:, None, None] * modulus[None]
    diag_salt = 1.0 + saline_mixing_rates[:, None, None] * modulus[None]
    cross_term = cross_mixing_rates[:, None, None] * modulus[None]
    determinant = diag_temp * diag_salt + cross_term * cross_term
    new_temp_real = (diag_salt * heat_nonimag_share - cross_term * salt_real) / determinant
    new_temp_imag = (diag_salt * temp_imag - cross_term * salt_imag) / determinant
    new_salt_real = (diag_temp * salt_real + cross_term * heat_nonimag_share) / determinant
    new_salt_imag = (diag_temp * salt_imag + cross_term * temp_imag) / determinant
    temp_x_real, temp_x_imag = inverse_x(new_temp_real, new_temp_imag)
    salt_x_real, salt_x_imag = inverse_x(new_salt_real, new_salt_imag)
    pieces = (
        lax.all_to_all(temp_x_real, "hor", split_axis=1, concat_axis=1, tiled=True),
        lax.all_to_all(temp_x_imag, "hor", split_axis=1, concat_axis=1, tiled=True),
        lax.all_to_all(salt_x_real, "hor", split_axis=1, concat_axis=1, tiled=True),
        lax.all_to_all(salt_x_imag, "hor", split_axis=1, concat_axis=1, tiled=True),
    )
    count = pieces[0].shape[0]
    shaped = [piece.reshape(count, parts, number_of_lines, slot_count) for piece in pieces]
    heat_nonimag_share = contract("zbxj,ybj->zxy", shaped[0], north_cos_lookup) - contract(
        "zbxj,ybj->zxy", shaped[1], north_sin_lookup
    )
    salt_real = contract("zbxj,ybj->zxy", shaped[2], north_cos_lookup) - contract(
        "zbxj,ybj->zxy", shaped[3], north_sin_lookup
    )
    filtered_heat_field = heat_nonimag_share * normalizing_factor
    filtered_saline_field = salt_real * normalizing_factor
    joined_layers = jnp.stack([filtered_heat_field, filtered_saline_field, updraft_speed])
    extended = extended_2(joined_layers, (("lev", 1),), 1)
    lower = extended[:, :-1]
    upper = extended[:, 1:]
    interface_flow = 0.5 * (lower[2] + upper[2]) + buoyancy * 0.5 * (
        lower[0] + upper[0] - (lower[1] + upper[1])
    )
    face_global = lax.axis_index("lev") * number_of_layers + jnp.arange(number_of_layers + 1) - 1
    total_levels = number_of_layers * lax.axis_size("lev")
    open_face = ((face_global >= 0) & (face_global <= total_levels - 2))[:, None, None]
    upward_flow = jnp.maximum(interface_flow, 0.0)
    downward_flow = jnp.minimum(interface_flow, 0.0)
    heat_transport = jnp.where(open_face, upward_flow * lower[0] + downward_flow * upper[0], 0.0)
    flux_salt = jnp.where(open_face, upward_flow * lower[1] + downward_flow * upper[1], 0.0)
    updated_heat_field = filtered_heat_field - advective_number * (
        heat_transport[1:] - heat_transport[:-1]
    )
    salt_out = filtered_saline_field - advective_number * (flux_salt[1:] - flux_salt[:-1])
    return (updated_heat_field, salt_out)


def solution(mesh):
    in_specs = (
        P("lev", "hor", None),
        P("lev", "hor", None),
        P("lev", "hor", None),
        P("lev"),
        P("lev"),
        P("lev"),
    )
    out_specs = (P("lev", "hor", None), P("lev", "hor", None))
    return jax.shard_map(shards, mesh=mesh, in_specs=in_specs, out_specs=out_specs, check_vma=False)
```

profile of v0, /device:TPU:34, one launch (start us, length us, event | category | flops | bytes accessed | tf_op | source)
XLA Modules:
  0.0 419.6 jit_solution(3036475040510812166)
XLA Ops:
  0.7 17.5 %convolution_multiply_fusion = f32[32,16,32,16]{2,1,3,0:T(8,128)} fusion(f32[32,16,512]{2,1,0:T(8,128)} %param.7, s32[32,16]{1,0:T(8,128)S(1)} %copy.54), kind=kOutput, calls=%fused_computation.15 | convolution fusion | flops 1614544896 | bytes 2099200 | tf_op jit(solution)/shard_map/uhq,qvj->uvhj/dot_general | solution.py:44
  18.2 3.7 copy.68
  21.9 11.1 %all-to-all-start.3 = ((f32[32,32,256]{2,0,1:T(8,128)}), f32[32,32,256]{2,0,1:T(8,128)S(1)}, u32[]{:S(2)}, u32[]{:S(2)}) async-start(f32[32,32,256]{2,0,1:T(8,128)} %copy.68), calls=%async_computation.3 | async-start | bytes 2097152 | tf_op jit(solution)/shard_map/all_to_all | solution.py:114
  33.0 12.7 %fusion.72 = f32[32,16,32,16]{2,1,3,0:T(8,128)} fusion(f32[32,16,512]{2,1,0:T(8,128)S(1)} %copy-done.7, s32[32,16]{1,0:T(8,128)S(1)} %copy.54), kind=kOutput, calls=%fused_computation.91 | convolution fusion | flops 1614282752 | bytes 2099200 | tf_op jit(solution)/shard_map/uhq,qvj->uvhj/dot_general | solution.py:44
  45.7 3.7 copy.64
  49.4 11.8 %all-to-all-done.3 = f32[32,32,256]{2,0,1:T(8,128)S(1)} async-done(((f32[32,32,256]{2,0,1:T(8,128)}), f32[32,32,256]{2,0,1:T(8,128)S(1)}, u32[]{:S(2)}, u32[]{:S(2)}) %all-to-all-start.3) | async-done | bytes 1048608 | tf_op jit(solution)/shard_map/all_to_all | solution.py:114
  61.3 5.8 %all-to-all-start.2 = ((f32[32,32,256]{2,0,1:T(8,128)}), f32[32,32,256]{2,0,1:T(8,128)S(1)}, u32[]{:S(2)}, u32[]{:S(2)}) async-start(f32[32,32,256]{2,0,1:T(8,128)} %copy.64), calls=%async_computation.2 | async-start | bytes 2097152 | tf_op jit(solution)/shard_map/all_to_all | solution.py:111
  67.1 12.7 %fusion.75 = f32[32,16,32,16]{2,1,3,0:T(8,128)} fusion(f32[32,16,512]{2,1,0:T(8,128)S(1)} %copy-done.8, s32[32,16]{1,0:T(8,128)S(1)} %copy.54), kind=kOutput, calls=%fused_computation.94 | convolution fusion | flops 1614282752 | bytes 2099200 | tf_op jit(solution)/shard_map/uhq,qvj->uvhj/dot_general | solution.py:44
  79.8 3.6 copy.56
  83.4 6.7 %all-to-all-done.2 = f32[32,32,256]{2,0,1:T(8,128)S(1)} async-done(((f32[32,32,256]{2,0,1:T(8,128)}), f32[32,32,256]{2,0,1:T(8,128)S(1)}, u32[]{:S(2)}, u32[]{:S(2)}) %all-to-all-start.2) | async-done | bytes 1048608 | tf_op jit(solution)/shard_map/all_to_all | solution.py:111
  90.0 11.2 %all-to-all-start = ((f32[32,32,256]{2,0,1:T(8,128)}), f32[32,32,256]{2,0,1:T(8,128)S(1)}, u32[]{:S(2)}, u32[]{:S(2)}) async-start(f32[32,32,256]{2,0,1:T(8,128)} %copy.56), calls=%async_computation | async-start | bytes 2097152 | tf_op jit(solution)/shard_map/all_to_all | solution.py:105
  101.2 17.5 %convolution_multiply_fusion.1 = f32[32,16,32,16]{2,1,3,0:T(8,128)} fusion(f32[32,16,512]{2,1,0:T(8,128)} %param.6, s32[32,16]{1,0:T(8,128)S(1)} %copy.54), kind=kOutput, calls=%fused_computation.16 | convolution fusion | flops 1614544896 | bytes 2099200 | tf_op jit(solution)/shard_map/uhq,qvj->uvhj/dot_general | solution.py:44
  118.7 3.6 copy.60
  122.3 1.7 all-to-all-done
  125.0 11.2 %all-to-all-start.1 = ((f32[32,32,256]{2,0,1:T(8,128)}), f32[32,32,256]{2,0,1:T(8,128)S(1)}, u32[]{:S(2)}, u32[]{:S(2)}) async-start(f32[32,32,256]{2,0,1:T(8,128)} %copy.60), calls=%async_computation.1 | async-start | bytes 2097152 | tf_op jit(solution)/shard_map/all_to_all | solution.py:108
  136.4 2.7 copy.69
  139.1 3.9 copy.70
  142.9 2.7 copy.65
  145.6 4.0 copy.66
  149.6 2.7 copy.57
  152.2 3.3 copy.58
  155.6 6.3 %fusion.93 = f32[32,16,512]{2,1,0:T(8,128)S(1)} fusion(f32[32,512,16]{1,2,0:T(8,128)S(1)} %copy-done.5), kind=kOutput, calls=%fused_computation.112 | convolution fusion | flops 1614282752 | bytes 2097152 | tf_op jit(solution)/shard_map/zxj,xm->zjm/dot_general | solution.py:44
  161.9 6.3 %fusion.99 = f32[32,16,512]{2,1,0:T(8,128)S(1)} fusion(f32[32,512,16]{1,2,0:T(8,128)S(1)} %copy-done.6), kind=kOutput, calls=%fused_computation.118 | convolution fusion | flops 1614282752 | bytes 2097152 | tf_op jit(solution)/shard_map/zxj,xm->zjm/dot_general | solution.py:44
  168.2 7.1 %fusion.101 = f32[32,16,512]{2,1,0:T(8,128)} fusion(f32[32,512,16]{1,2,0:T(8,128)S(1)} %copy.58), kind=kOutput, calls=%fused_computation.120 | convolution fusion | flops 1614282752 | bytes 2097152 | tf_op jit(solution)/shard_map/zxj,xm->zjm/dot_general | solution.py:44
  175.3 6.7 %fusion.24 = f32[32,16,512]{2,1,0:T(8,128)} fusion(f32[32,16,512]{2,1,0:T(8,128)S(1)} %fusion.93, f32[32,512,16]{1,2,0:T(8,128)S(1)} %copy-done.6), kind=kOutput, calls=%fused_computation.39 | convolution fusion | flops 1614807040 | bytes 3145728 | tf_op jit(solution)/shard_map/zxj,xm->zjm/dot_general | solution.py:44
  182.0 6.7 %fusion.26 = f32[32,16,512]{2,1,0:T(8,128)} fusion(f32[32,16,512]{2,1,0:T(8,128)S(1)} %fusion.99, f32[32,512,16]{1,2,0:T(8,128)S(1)} %copy-done.5), kind=kOutput, calls=%fused_computation.43 | convolution fusion | flops 1614807040 | bytes 3145728 | tf_op jit(solution)/shard_map/zxj,xm->zjm/dot_general | solution.py:44
  188.6 2.7 copy.61
  191.3 3.2 copy.62
  194.5 6.5 %fusion.95 = f32[32,16,512]{2,1,0:T(8,128)S(1)} fusion(f32[32,512,16]{1,2,0:T(8,128)S(1)} %copy.62), kind=kOutput, calls=%fused_computation.114 | convolution fusion | flops 1614282752 | bytes 2097152 | tf_op jit(solution)/shard_map/zxj,xm->zjm/dot_general | solution.py:44
  201.1 6.3 %fusion.27 = f32[32,16,512]{2,1,0:T(8,128)S(1)} fusion(f32[32,16,512]{2,1,0:T(8,128)S(1)} %copy-done.21, f32[32,512,16]{1,2,0:T(8,128)S(1)} %copy.62), kind=kOutput, calls=%fused_computation.45 | convolution fusion | flops 1614807040 | bytes 3145728 | tf_op jit(solution)/shard_map/zxj,xm->zjm/dot_general | solution.py:44
  207.5 8.6 %fusion.60 = (f32[32,16,512]{2,1,0:T(8,128)S(1)}, f32[32,16,512]{2,1,0:T(8,128)}, f32[32,16,512]{2,1,0:T(8,128)}, f32[32,16,512]{2,1,0:T(8,128)S(1)}) fusion(f32[32,16,512]{2,1,0:T(8,128)S(1)} %copy-done.19, f32[32]{0:T(128)S(1)} %copy-done.9, f32[32]{0:T(128)S(1)} %copy-done.10, f32[16,512]{1,0:T(8,128)S(1)} %add_multiply_fusion, f32[32]{0:T(128)S(1)} %copy-done.11, ...), kind=kOutput, calls=%fused_computation.77 | convolution fusion | flops 1621098496 | bytes 9470336 | tf_op jit(solution)/shard_map/zxj,xm->zjm/dot_general | solution.py:44
  216.1 7.1 %fusion.89 = f32[512,32,16]{0,1,2:T(8,128)S(1)} fusion(f32[32,16,512]{2,1,0:T(8,128)S(1)} %get-tuple-element.13), kind=kOutput, calls=%fused_computation.108 | convolution fusion | flops 1614282752 | bytes 2097152 | tf_op jit(solution)/shard_map/zjm,mx->zxj/dot_general | solution.py:44
  223.2 7.0 %fusion.21 = f32[32,512,16]{1,0,2:T(8,128)S(1)} fusion(f32[512,32,16]{0,1,2:T(8,128)S(1)} %fusion.89, f32[32,16,512]{2,1,0:T(8,128)S(1)} %get-tuple-element.8), kind=kOutput, calls=%fused_computation.33 | convolution fusion | flops 1614544896 | bytes 3145728 | tf_op jit(solution)/shard_map/zjm,mx->zxj/dot_general | solution.py:44
  230.3 3.7 copy.89
  234.0 3.7 copy.90
  237.7 10.3 %all-to-all-start.6 = ((f32[32,32,256]{2,0,1:T(8,128)}), f32[32,32,256]{2,0,1:T(8,128)S(1)}, u32[]{:S(2)}, u32[]{:S(2)}) async-start(f32[32,32,256]{2,0,1:T(8,128)} %copy.90), calls=%async_computation.6 | async-start | bytes 2097152 | tf_op jit(solution)/shard_map/all_to_all | solution.py:139
  248.0 6.9 %fusion.87 = f32[512,32,16]{0,1,2:T(8,128)S(1)} fusion(f32[32,16,512]{2,1,0:T(8,128)S(1)} %copy-done.18), kind=kOutput, calls=%fused_computation.106 | convolution fusion | flops 1614282752 | bytes 2097152 | tf_op jit(solution)/shard_map/zjm,mx->zxj/dot_general | solution.py:44
  255.0 7.0 %fusion.20 = f32[32,512,16]{1,0,2:T(8,128)S(1)} fusion(f32[512,32,16]{0,1,2:T(8,128)S(1)} %fusion.87, f32[32,16,512]{2,1,0:T(8,128)S(1)} %copy-done.16), kind=kOutput, calls=%fused_computation.31 | convolution fusion | flops 1614544896 | bytes 3145728 | tf_op jit(solution)/shard_map/zjm,mx->zxj/dot_general | solution.py:44
  262.0 3.7 copy.95
  265.7 3.7 copy.96
  270.8 11.5 %all-to-all-start.7 = ((f32[32,32,256]{2,0,1:T(8,128)}), f32[32,32,256]{2,0,1:T(8,128)S(1)}, u32[]{:S(2)}, u32[]{:S(2)}) async-start(f32[32,32,256]{2,0,1:T(8,128)} %copy.96), calls=%async_computation.7 | async-start | bytes 2097152 | tf_op jit(solution)/shard_map/all_to_all | solution.py:140
  282.4 6.9 %fusion.97 = f32[512,32,16]{0,1,2:T(8,128)S(1)} fusion(f32[32,16,512]{2,1,0:T(8,128)S(1)} %copy-done.12), kind=kOutput, calls=%fused_computation.116 | convolution fusion | flops 1614282752 | bytes 2097152 | tf_op jit(solution)/shard_map/zjm,mx->zxj/dot_general | solution.py:44
  289.3 7.0 %fusion.23 = f32[32,512,16]{1,0,2:T(8,128)S(1)} fusion(f32[512,32,16]{0,1,2:T(8,128)S(1)} %fusion.97, f32[32,16,512]{2,1,0:T(8,128)S(1)} %copy-done.14), kind=kOutput, calls=%fused_computation.37 | convolution fusion | flops 1614544896 | bytes 3145728 | tf_op jit(solution)/shard_map/zjm,mx->zxj/dot_general | solution.py:44
  296.3 3.7 copy.77
  300.0 3.6 copy.78
  303.7 1.5 all-to-all-done.7
  305.2 11.2 %all-to-all-start.4 = ((f32[32,32,256]{2,0,1:T(8,128)}), f32[32,32,256]{2,0,1:T(8,128)S(1)}, u32[]{:S(2)}, u32[]{:S(2)}) async-start(f32[32,32,256]{2,0,1:T(8,128)} %copy.78), calls=%async_computation.4 | async-start | bytes 2097152 | tf_op jit(solution)/shard_map/all_to_all | solution.py:137
  316.4 8.2 %fusion.91 = f32[512,32,16]{0,1,2:T(8,128)S(1)} fusion(f32[32,16,512]{2,1,0:T(8,128)} %get-tuple-element.9), kind=kOutput, calls=%fused_computation.110 | convolution fusion | flops 1614282752 | bytes 2097152 | tf_op jit(solution)/shard_map/zjm,mx->zxj/dot_general | solution.py:44
  324.7 7.4 %fusion.22 = f32[32,512,16]{1,0,2:T(8,128)} fusion(f32[512,32,16]{0,1,2:T(8,128)S(1)} %fusion.91, f32[32,16,512]{2,1,0:T(8,128)S(1)} %copy-done.13), kind=kOutput, calls=%fused_computation.35 | convolution fusion | flops 1614544896 | bytes 3145728 | tf_op jit(solution)/shard_map/zjm,mx->zxj/dot_general | solution.py:44
  332.0 4.6 %copy.83 = f32[32,512,16]{0,2,1:T(8,128)} copy(f32[32,512,16]{1,0,2:T(8,128)} %fusion.22) | data formatting | bytes 2097152 | tf_op jit(solution)/shard_map/add | solution.py:49
  336.7 3.6 copy.84
  340.3 10.0 %all-to-all-start.5 = ((f32[32,32,256]{2,0,1:T(8,128)}), f32[32,32,256]{2,0,1:T(8,128)}, u32[]{:S(2)}, u32[]{:S(2)}) async-start(f32[32,32,256]{2,0,1:T(8,128)} %copy.84), calls=%async_computation.5 | async-start | bytes 2097152 | tf_op jit(solution)/shard_map/all_to_all | solution.py:138
  350.3 2.7 copy.91
  353.0 2.7 copy.97
  355.7 2.9 copy.79
  358.6 10.5 %fusion.14 = f32[32,16,512]{2,1,0:T(8,128)S(1)} fusion(f32[32,32,16,16]{1,3,2,0:T(8,128)} %bitcast.185, s32[32,16]{0,1:T(8,128)S(1)} %fusion.156), kind=kOutput, calls=%fused_computation.28 | convolution fusion | flops 1614282752 | bytes 2099200 | tf_op jit(solution)/shard_map/zbxj,ybj->zxy/dot_general | solution.py:44
  369.1 8.6 %fusion.8 = f32[32,16,512]{2,1,0:T(8,128)S(1)} fusion(f32[32,32,16,16]{1,3,2,0:T(8,128)S(1)} %bitcast.186, s32[32,16]{0,1:T(8,128)S(1)} %fusion.156), kind=kOutput, calls=%fused_computation.26 | convolution fusion | flops 1614282752 | bytes 2099200 | tf_op jit(solution)/shard_map/zbxj,ybj->zxy/dot_general | solution.py:44
  377.7 8.4 %fusion.31 = f32[32,16,512]{2,1,0:T(8,128)S(1)} fusion(f32[32,16,512]{2,1,0:T(8,128)S(1)} %fusion.14, f32[32,32,16,16]{1,3,2,0:T(8,128)S(1)} %bitcast.184, s32[32,16]{0,1:T(8,128)S(1)} %fusion.156), kind=kOutput, calls=%fused_computation.47 | convolution fusion | flops 1614807040 | bytes 3147776 | tf_op jit(solution)/shard_map/zbxj,ybj->zxy/dot_general | solution.py:44
  386.1 3.6 copy.85
  389.8 10.4 %fusion.37 = f32[32,16,512]{2,1,0:T(8,128)S(1)} fusion(f32[32,16,512]{2,1,0:T(8,128)S(1)} %fusion.8, f32[32,32,16,16]{1,3,2,0:T(8,128)} %bitcast.187, s32[32,16]{0,1:T(8,128)S(1)} %fusion.156), kind=kOutput, calls=%fused_computation.49 | convolution fusion | flops 1614807040 | bytes 3147776 | tf_op jit(solution)/shard_map/zbxj,ybj->zxy/dot_general | solution.py:44
  400.2 6.3 %collective-permute-start.1 = (f32[3,1,16,512]{3,2,1,0:T(8,128)S(1)}, f32[3,1,16,512]{3,2,1,0:T(8,128)S(1)}, u32[]{:S(2)}, u32[]{:S(2)}) collective-permute-start(f32[3,1,16,512]{3,2,1,0:T(8,128)S(1)} %get-tuple-element.6), channel_id=1, source_target_pairs={{32,0},{64,32},{96,64},{128,96},{160,128},{192,160},{224,192},{33,... | collective-permute-start | bytes 294920 | tf_op jit(solution)/shard_map/ppermute | solution.py:21
  406.6 1.9 collective-permute-start
  408.9 6.3 %collective-permute-done = f32[3,1,16,512]{3,2,1,0:T(8,128)S(1)} collective-permute-done((f32[3,1,16,512]{3,2,1,0:T(8,128)S(1)}, f32[3,1,16,512]{3,2,1,0:T(8,128)S(1)}, u32[]{:S(2)}, u32[]{:S(2)}) %collective-permute-start) | collective-permute-done | bytes 98336 | tf_op jit(solution)/shard_map/ppermute | solution.py:18
  417.6 1.8 fusion.62
  (59 shorter events, 5.5 us)
Async XLA Ops:
  18.2 14.8 %copy-start.7 = (f32[32,16,512]{2,1,0:T(8,128)S(1)}, f32[32,16,512]{2,1,0:T(8,128)}, u32[]{:S(2)}) copy-start(f32[32,16,512]{2,1,0:T(8,128)} %param.7) | copy-start | bytes 3145732
  21.9 39.4 %all-to-all-start.3 = ((f32[32,32,256]{2,0,1:T(8,128)}), f32[32,32,256]{2,0,1:T(8,128)S(1)}, u32[]{:S(2)}, u32[]{:S(2)}) async-start(f32[32,32,256]{2,0,1:T(8,128)} %copy.68), calls=%async_computation.3 | async-start | bytes 2097152 | tf_op jit(solution)/shard_map/all_to_all | solution.py:114
  45.7 21.3 %copy-start.8 = (f32[32,16,512]{2,1,0:T(8,128)S(1)}, f32[32,16,512]{2,1,0:T(8,128)}, u32[]{:S(2)}) copy-start(f32[32,16,512]{2,1,0:T(8,128)} %param.6) | copy-start | bytes 3145732
  61.3 28.8 %all-to-all-start.2 = ((f32[32,32,256]{2,0,1:T(8,128)}), f32[32,32,256]{2,0,1:T(8,128)S(1)}, u32[]{:S(2)}, u32[]{:S(2)}) async-start(f32[32,32,256]{2,0,1:T(8,128)} %copy.64), calls=%async_computation.2 | async-start | bytes 2097152 | tf_op jit(solution)/shard_map/all_to_all | solution.py:111
  90.0 34.0 %all-to-all-start = ((f32[32,32,256]{2,0,1:T(8,128)}), f32[32,32,256]{2,0,1:T(8,128)S(1)}, u32[]{:S(2)}, u32[]{:S(2)}) async-start(f32[32,32,256]{2,0,1:T(8,128)} %copy.56), calls=%async_computation | async-start | bytes 2097152 | tf_op jit(solution)/shard_map/all_to_all | solution.py:105
  124.0 1.0 copy-start.3
  125.0 63.6 %all-to-all-start.1 = ((f32[32,32,256]{2,0,1:T(8,128)}), f32[32,32,256]{2,0,1:T(8,128)S(1)}, u32[]{:S(2)}, u32[]{:S(2)}) async-start(f32[32,32,256]{2,0,1:T(8,128)} %copy.60), calls=%async_computation.1 | async-start | bytes 2097152 | tf_op jit(solution)/shard_map/all_to_all | solution.py:108
  145.6 4.0 copy-start.4
  152.2 3.3 copy-start.5
  155.6 6.3 %copy-start.6 = (f32[32,512,16]{1,2,0:T(8,128)S(1)}, f32[32,512,16]{1,2,0:T(8,128)}, u32[]{:S(2)}) copy-start(f32[32,512,16]{1,2,0:T(8,128)} %copy.66) | copy-start | bytes 3145732
  194.5 6.5 %copy-start.21 = (f32[32,16,512]{2,1,0:T(8,128)S(1)}, f32[32,16,512]{2,1,0:T(8,128)}, u32[]{:S(2)}) copy-start(f32[32,16,512]{2,1,0:T(8,128)} %fusion.101) | copy-start | bytes 3145732
  201.1 6.4 %copy-start.9 = (f32[32]{0:T(128)S(1)}, f32[32]{0:T(128)}, u32[]{:S(2)}) copy-start(f32[32]{0:T(128)} %param.9) | copy-start | bytes 388
  201.1 6.4 %copy-start.10 = (f32[32]{0:T(128)S(1)}, f32[32]{0:T(128)}, u32[]{:S(2)}) copy-start(f32[32]{0:T(128)} %param.11) | copy-start | bytes 388
  201.1 6.4 %copy-start.11 = (f32[32]{0:T(128)S(1)}, f32[32]{0:T(128)}, u32[]{:S(2)}) copy-start(f32[32]{0:T(128)} %param.10) | copy-start | bytes 388
  201.1 6.4 %copy-start.19 = (f32[32,16,512]{2,1,0:T(8,128)S(1)}, f32[32,16,512]{2,1,0:T(8,128)}, u32[]{:S(2)}) copy-start(f32[32,16,512]{2,1,0:T(8,128)} %fusion.24) | copy-start | bytes 3145732
  201.1 6.4 %copy-start.20 = (f32[32,16,512]{2,1,0:T(8,128)S(1)}, f32[32,16,512]{2,1,0:T(8,128)}, u32[]{:S(2)}) copy-start(f32[32,16,512]{2,1,0:T(8,128)} %fusion.26) | copy-start | bytes 3145732
  216.1 7.1 %copy-start.17 = (f32[32,16,512]{2,1,0:T(8,128)}, f32[32,16,512]{2,1,0:T(8,128)S(1)}, u32[]{:S(2)}) copy-start(f32[32,16,512]{2,1,0:T(8,128)S(1)} %get-tuple-element.8) | copy-start | bytes 3145732
  216.1 14.2 %copy-start.15 = (f32[32,16,512]{2,1,0:T(8,128)}, f32[32,16,512]{2,1,0:T(8,128)S(1)}, u32[]{:S(2)}) copy-start(f32[32,16,512]{2,1,0:T(8,128)S(1)} %get-tuple-element.13) | copy-start | bytes 3145732
  234.0 14.1 %copy-start.18 = (f32[32,16,512]{2,1,0:T(8,128)S(1)}, f32[32,16,512]{2,1,0:T(8,128)}, u32[]{:S(2)}) copy-start(f32[32,16,512]{2,1,0:T(8,128)} %copy-done.17) | copy-start | bytes 3145732
  237.7 17.3 %copy-start.16 = (f32[32,16,512]{2,1,0:T(8,128)S(1)}, f32[32,16,512]{2,1,0:T(8,128)}, u32[]{:S(2)}) copy-start(f32[32,16,512]{2,1,0:T(8,128)} %copy-done.15) | copy-start | bytes 3145732
  237.7 33.1 %all-to-all-start.6 = ((f32[32,32,256]{2,0,1:T(8,128)}), f32[32,32,256]{2,0,1:T(8,128)S(1)}, u32[]{:S(2)}, u32[]{:S(2)}) async-start(f32[32,32,256]{2,0,1:T(8,128)} %copy.90), calls=%async_computation.6 | async-start | bytes 2097152 | tf_op jit(solution)/shard_map/all_to_all | solution.py:139
  265.7 16.7 %copy-start.12 = (f32[32,16,512]{2,1,0:T(8,128)S(1)}, f32[32,16,512]{2,1,0:T(8,128)}, u32[]{:S(2)}) copy-start(f32[32,16,512]{2,1,0:T(8,128)} %get-tuple-element.12) | copy-start | bytes 3145732
  270.8 34.3 %all-to-all-start.7 = ((f32[32,32,256]{2,0,1:T(8,128)}), f32[32,32,256]{2,0,1:T(8,128)S(1)}, u32[]{:S(2)}, u32[]{:S(2)}) async-start(f32[32,32,256]{2,0,1:T(8,128)} %copy.96), calls=%async_computation.7 | async-start | bytes 2097152 | tf_op jit(solution)/shard_map/all_to_all | solution.py:140
  282.4 7.0 %copy-start.14 = (f32[32,16,512]{2,1,0:T(8,128)S(1)}, f32[32,16,512]{2,1,0:T(8,128)}, u32[]{:S(2)}) copy-start(f32[32,16,512]{2,1,0:T(8,128)} %get-tuple-element.9) | copy-start | bytes 3145732
  305.2 35.1 %all-to-all-start.4 = ((f32[32,32,256]{2,0,1:T(8,128)}), f32[32,32,256]{2,0,1:T(8,128)S(1)}, u32[]{:S(2)}, u32[]{:S(2)}) async-start(f32[32,32,256]{2,0,1:T(8,128)} %copy.78), calls=%async_computation.4 | async-start | bytes 2097152 | tf_op jit(solution)/shard_map/all_to_all | solution.py:137
  316.4 8.2 %copy-start.13 = (f32[32,16,512]{2,1,0:T(8,128)S(1)}, f32[32,16,512]{2,1,0:T(8,128)}, u32[]{:S(2)}) copy-start(f32[32,16,512]{2,1,0:T(8,128)} %get-tuple-element.12) | copy-start | bytes 3145732
  340.3 45.8 %all-to-all-start.5 = ((f32[32,32,256]{2,0,1:T(8,128)}), f32[32,32,256]{2,0,1:T(8,128)}, u32[]{:S(2)}, u32[]{:S(2)}) async-start(f32[32,32,256]{2,0,1:T(8,128)} %copy.84), calls=%async_computation.5 | async-start | bytes 2097152 | tf_op jit(solution)/shard_map/all_to_all | solution.py:138
  358.6 10.5 %copy-start.2 = (f32[32,32,256]{1,2,0:T(8,128)S(1)}, f32[32,32,256]{1,2,0:T(8,128)}, u32[]{:S(2)}) copy-start(f32[32,32,256]{1,2,0:T(8,128)} %copy.79) | copy-start | bytes 3145732
  369.1 8.6 %copy-start.1 = (f32[32,32,256]{1,2,0:T(8,128)S(1)}, f32[32,32,256]{1,2,0:T(8,128)}, u32[]{:S(2)}) copy-start(f32[32,32,256]{1,2,0:T(8,128)} %copy.97) | copy-start | bytes 3145732
  389.8 10.4 %copy-start = (f32[32,16,512]{2,1,0:T(8,128)S(1)}, f32[32,16,512]{2,1,0:T(8,128)}, u32[]{:S(2)}) copy-start(f32[32,16,512]{2,1,0:T(8,128)} %param.8) | copy-start | bytes 3145732
  400.2 8.7 %collective-permute-start.1 = (f32[3,1,16,512]{3,2,1,0:T(8,128)S(1)}, f32[3,1,16,512]{3,2,1,0:T(8,128)S(1)}, u32[]{:S(2)}, u32[]{:S(2)}) collective-permute-start(f32[3,1,16,512]{3,2,1,0:T(8,128)S(1)} %get-tuple-element.6), channel_id=1, source_target_pairs={{32,0},{64,32},{96,64},{128,96},{160,128},{192,160},{224,192},{33,... | collective-permute-start | bytes 294920 | tf_op jit(solution)/shard_map/ppermute | solution.py:21
  406.6 8.6 %collective-permute-start = (f32[3,1,16,512]{3,2,1,0:T(8,128)S(1)}, f32[3,1,16,512]{3,2,1,0:T(8,128)S(1)}, u32[]{:S(2)}, u32[]{:S(2)}) collective-permute-start(f32[3,1,16,512]{3,2,1,0:T(8,128)S(1)} %get-tuple-element.7), channel_id=1, source_target_pairs={{0,32},{32,64},{64,96},{96,128},{128,160},{160,192},{192,224},{1,3... | collective-permute-start | bytes 294920 | tf_op jit(solution)/shard_map/ppermute | solution.py:18
where the time goes:
time: 427 us; the launch traced here: 420 us
  matrix products  210 us (49%)
  starting transfers between devices  90.6 us (21%)
  local copies, waits for them, and re-layouts  83.2 us (19%)
  waiting for transfers between devices  29.9 us (7%)
  other arithmetic  4.33 us (1%)
    dot_general x24, matrix products, contract(): return jnp.einsum(form, left, right, precision=highest)  210 us
    reshape x8, local copies, waits for them, and re-layouts, split_into_groups(): return array.reshape(number_of_layers, parts, number_of_lines * slot_count)  29.3 us
    reshape x4, local copies, waits for them, and re-layouts, shards(): shaped = [piece.reshape(count, length_x, slot_count) for piece in pieces]  14.4 us
    all_to_all x1, waiting for transfers between devices, shards(): lax.all_to_all(split_into_groups(salt_y_imag), 'hor', split_axis=1, conca...  11.8 us
    all_to_all x1, starting transfers between devices, shards(): lax.all_to_all(salt_x_imag, 'hor', split_axis=1, concat_axis=1, tiled=True)  11.5 us
    all_to_all x1, starting transfers between devices, shards(): lax.all_to_all(split_into_groups(heat_north_quadrature), 'hor', split_axi...  11.2 us
    all_to_all x1, starting transfers between devices, shards(): lax.all_to_all(temp_x_real, 'hor', split_axis=1, concat_axis=1, tiled=True)  11.2 us
    all_to_all x1, starting transfers between devices, shards(): lax.all_to_all(split_into_groups(heat_north_inphase), 'hor', split_axis=1...  11.2 us
  transfers between devices with their start and end apart: 10, of which 7 were waited for; matrix products, arithmetic and copies ran while one was open for 50% of the time, Pallas kernels for 0%

commit v1 on v0

v1 whole, which is shorter than its diff:
```python
import functools
import math

import jax
import jax.numpy as jnp
import numpy as np
from jax import lax
from jax.experimental import pallas as pl
from jax.experimental.pallas import tpu as pltpu
from jax.sharding import PartitionSpec as P

buoyancy = 0.5
advective_number = 0.25


def real_basis(length):
    half = length // 2
    points = np.arange(half)
    tables, waves = [], []
    for parity in (0, 1):
        cos_waves = np.arange(parity, half + 1, 2)
        sin_waves = np.array([k for k in cos_waves if 0 < k < half])
        rows = []
        for k in cos_waves:
            weight = math.sqrt((1.0 if k in (0, half) else 2.0) / length)
            rows.append(weight * np.cos(2.0 * math.pi / length * ((k * points) % length)))
        for k in sin_waves:
            rows.append(math.sqrt(2.0 / length) * np.sin(2.0 * math.pi / length * ((k * points) % length)))
        tables.append(np.stack(rows))
        waves.append(np.concatenate([cos_waves, sin_waves]))
    return tables, waves


def parts_of(table):
    kind = np.dtype(jnp.bfloat16)
    high = table.astype(kind)
    return high, (table - high.astype(np.float64)).astype(kind)


def split(value):
    high = value.astype(jnp.bfloat16)
    low = (value - high.astype(jnp.float32)).astype(jnp.bfloat16)
    return high, low


def dot(left, right):
    return jnp.dot(left, right, preferred_element_type=jnp.float32)


def right_product(value, table_high, table_low):
    high, low = split(value)
    return dot(high, table_high) + dot(low, table_high) + dot(high, table_low)


def left_product(table_high, table_low, value):
    high, low = split(value)
    return dot(table_high, high) + dot(table_low, high) + dot(table_high, low)


def spectral_kernel(rt_ref, rs_ref, rc_ref, x_ref, tab_ref, sq_ref, sqt_ref, out_ref):
    length = x_ref.shape[-1]
    half = length // 2
    level = lax.axis_index("hor")
    rate_t, rate_s, rate_c = rt_ref[level], rs_ref[level], rc_ref[level]

    def table(parity, transposed, low):
        return tab_ref[parity * 4 + transposed * 2 + low]

    def folded(field):
        value = x_ref[:, field].reshape(length, length)
        rows = (value[:half] + value[half:], value[:half] - value[half:])
        return [[r[:, :half] + r[:, half:], r[:, :half] - r[:, half:]] for r in rows]

    planes = [folded(0), folded(1)]
    inner = {}
    for q in (0, 1):
        stacked = jnp.concatenate([planes[f][p][q] for f in (0, 1) for p in (0, 1)], axis=0)
        product = right_product(stacked, table(q, 1, 0), table(q, 1, 1))
        for f in (0, 1):
            for p in (0, 1):
                at = (2 * f + p) * half
                inner[f, p, q] = product[at : at + half]
    back = {}
    for p in (0, 1):
        stacked = jnp.concatenate([inner[f, p, q] for f in (0, 1) for q in (0, 1)], axis=1)
        product = left_product(table(p, 0, 0), table(p, 0, 1), stacked)
        temp, salt = product[:, :length], product[:, length:]
        modulus = (sq_ref[:, p : p + 1] + sqt_ref[...]) / ((length / 2.0) * (length / 2.0))
        diag_temp = 1.0 + rate_t * modulus
        diag_salt = 1.0 + rate_s * modulus
        cross = rate_c * modulus
        determinant = diag_temp * diag_salt + cross * cross
        new_temp = (diag_salt * temp - cross * salt) / determinant
        new_salt = (diag_temp * salt + cross * temp) / determinant
        product = left_product(
            table(p, 1, 0), table(p, 1, 1), jnp.concatenate([new_temp, new_salt], axis=1)
        )
        for f in (0, 1):
            for q in (0, 1):
                at = (2 * f + q) * half
                back[f, p, q] = product[:, at : at + half]
    result = {}
    for q in (0, 1):
        stacked = jnp.concatenate([back[f, p, q] for f in (0, 1) for p in (0, 1)], axis=0)
        product = right_product(stacked, table(q, 0, 0), table(q, 0, 1))
        for f in (0, 1):
            for p in (0, 1):
                at = (2 * f + p) * half
                result[f, p, q] = product[at : at + half]
    blocks = x_ref.shape[0] // 2
    shape = (blocks,) + x_ref.shape[2:3] + (half,)
    for f in (0, 1):
        rows = [(result[f, p, 0] + result[f, p, 1], result[f, p, 0] - result[f, p, 1]) for p in (0, 1)]
        for side in (0, 1):
            columns = slice(side * half, (side + 1) * half)
            out_ref[:blocks, f, :, columns] = (rows[0][side] + rows[1][side]).reshape(shape)
            out_ref[blocks:, f, :, columns] = (rows[0][side] - rows[1][side]).reshape(shape)


def spectral_step(x, rate_t, rate_s, rate_c):
    length = x.shape[-1]
    tables, waves = real_basis(length)
    stack = []
    for table in tables:
        for oriented in (table, table.T):
            stack.extend(parts_of(oriented))
    squares = np.stack([w.astype(np.float32) ** 2 for w in waves], axis=1)
    vmem = pl.BlockSpec(memory_space=pltpu.VMEM)
    smem = pl.BlockSpec(memory_space=pltpu.SMEM)
    return pl.pallas_call(
        spectral_kernel,
        out_shape=jax.ShapeDtypeStruct(x.shape, jnp.float32),
        in_specs=[smem] * 3 + [vmem] * 4,
        out_specs=vmem,
        compiler_params=pltpu.CompilerParams(vmem_limit_bytes=40 << 20),
        name="spectral",
    )(
        rate_t,
        rate_s,
        rate_c,
        x,
        jnp.asarray(np.stack(stack)),
        jnp.asarray(squares),
        jnp.asarray(np.concatenate([squares[:, 0], squares[:, 1]])[None, :]),
    )


def flux_kernel(u_ref, w_ref, low_ref, high_ref, wlow_ref, whigh_ref, t_out, s_out):
    levels = u_ref.shape[0]
    block = lax.axis_index("lev")
    last = lax.axis_size("lev") - 1

    def face(lt, ls, lw, ut, us, uw):
        flow = 0.5 * (lw + uw) + buoyancy * 0.5 * ((lt + ut) - (ls + us))
        up = jnp.maximum(flow, 0.0)
        down = jnp.minimum(flow, 0.0)
        return up * lt + down * ut, up * ls + down * us

    at = (u_ref[0, 0], u_ref[0, 1], w_ref[0])
    below = face(low_ref[0], low_ref[1], wlow_ref[...], *at)
    open_low = block > 0
    below = tuple(jnp.where(open_low, b, 0.0) for b in below)
    for level in range(levels):
        if level + 1 < levels:
            nxt = (u_ref[level + 1, 0], u_ref[level + 1, 1], w_ref[level + 1])
            above = face(*at, *nxt)
        else:
            nxt = None
            above = face(*at, high_ref[0], high_ref[1], whigh_ref[...])
            above = tuple(jnp.where(block < last, a, 0.0) for a in above)
        t_out[level] = at[0] - advective_number * (above[0] - below[0])
        s_out[level] = at[1] - advective_number * (above[1] - below[1])
        at, below = nxt, above


def shards(heat, saline, updraft, rate_t, rate_s, rate_c):
    count = lax.axis_size("lev")
    upward = [(i, i + 1) for i in range(count - 1)]
    downward = [(i + 1, i) for i in range(count - 1)]
    w_low = lax.ppermute(updraft[-1], "lev", upward)
    w_high = lax.ppermute(updraft[0], "lev", downward)
    both = jnp.stack([heat, saline], axis=1)
    whole = lax.all_to_all(both, "hor", split_axis=0, concat_axis=0, tiled=True)
    solved = spectral_step(whole, rate_t, rate_s, rate_c)
    filtered = lax.all_to_all(solved, "hor", split_axis=0, concat_axis=0, tiled=True)
    low = lax.ppermute(filtered[-1], "lev", upward)
    high = lax.ppermute(filtered[0], "lev", downward)
    vmem = pl.BlockSpec(memory_space=pltpu.VMEM)
    shape = jax.ShapeDtypeStruct(heat.shape, jnp.float32)
    return pl.pallas_call(
        flux_kernel,
        out_shape=(shape, shape),
        in_specs=[vmem] * 6,
        out_specs=(vmem, vmem),
        name="flux",
    )(filtered, updraft, low, high, w_low, w_high)


def solution(mesh):
    field = P("lev", "hor", None)
    return jax.shard_map(
        shards,
        mesh=mesh,
        in_specs=(field,) * 3 + (P("lev"),) * 3,
        out_specs=(field, field),
        check_vma=False,
    )
```

time: 427 us -> 152 us (0.36); the launches traced: 420 us -> 152 us
  matrix products: 210 us -> 0 us
  blocking collectives: 0 us -> 107 us
  local copies, waits for them, and re-layouts: 83.2 us -> 2.06 us
  starting transfers between devices: 90.6 us -> 26 us
  waiting for transfers between devices: 29.9 us -> 5.98 us
  Pallas kernels: 0 us -> 8.86 us
    dot_general x24 -> x0, matrix products: 210 us -> none  [contract(): return jnp.einsum(form, left, right, precision=highest)]
    all_to_all x0 -> x2, blocking collectives: none -> 107 us  [the longest x1 61.3 us: shards(): whole = lax.all_to_all(both, 'hor', split_axis=0, concat_axis=0, tiled=True)]
    all_to_all x8 -> x0, starting transfers between devices: 82.3 us -> none  [the longest x1 11.5 us: shards(): lax.all_to_all(salt_x_imag, 'hor', split_axis=1, concat_axis=1, tiled=True)]
    reshape x12 -> x0, local copies, waits for them, and re-layouts: 43.7 us -> none  [the longest x8 29.3 us: split_into_groups(): return array.reshape(number_of_layers, parts, number_of_lines * slot_count)]
    all_to_all x8 -> x0, waiting for transfers between devices: 23.2 us -> none  [the longest x1 11.8 us: shards(): lax.all_to_all(split_into_groups(salt_y_imag), 'hor', split_axis=1, conca...]
    all_to_all x8 -> x0, local copies, waits for them, and re-layouts: 22.6 us -> none  [the longest x1 3.65 us: shards(): lax.all_to_all(temp_x_imag, 'hor', split_axis=1, concat_axis=1, tiled=True)]
    ppermute x2 -> x4, starting transfers between devices: 8.26 us -> 26 us  [the longest x1 16.1 us: shards(): high = lax.ppermute(filtered[0], 'lev', downward)]
    pallas_call x0 -> x2, Pallas kernels: none -> 8.86 us  [the longest x1 4.82 us: spectral_step(): pl.pallas_call(spectral_kernel, out_shape=jax.ShapeDtypeStruct(x.shape, j...]
  transfers between devices with their start and end apart: 10 -> 4, of which waited for: 7 -> 1; matrix products, arithmetic and copies ran while one was open for 50% -> 1% of each run, Pallas kernels for 0% -> 0%
where the time goes in v1:
time: 152 us
  blocking collectives  107 us (70%)
  starting transfers between devices  26 us (17%)
  Pallas kernels  8.86 us (6%)
  waiting for transfers between devices  5.98 us (4%)
  local copies, waits for them, and re-layouts  2.06 us (1%)
  other arithmetic  1.8 us (1%)
    all_to_all x1, blocking collectives, shards(): whole = lax.all_to_all(both, 'hor', split_axis=0, concat_axis=0, tiled=True)  61.3 us
    all_to_all x1, blocking collectives, shards(): lax.all_to_all(solved, 'hor', split_axis=0, concat_axis=0, tiled=True)  45.3 us
    ppermute x1, starting transfers between devices, shards(): high = lax.ppermute(filtered[0], 'lev', downward)  16.1 us
    ppermute x1, starting transfers between devices, shards(): w_high = lax.ppermute(updraft[0], 'lev', downward)  6.02 us
    ppermute x1, waiting for transfers between devices, shards(): w_low = lax.ppermute(updraft[-1], 'lev', upward)  5.97 us
    pallas_call x1, Pallas kernels, spectral_step(): pl.pallas_call(spectral_kernel, out_shape=jax.ShapeDtypeStruct(x.shape, j...  4.82 us
    pallas_call x1, Pallas kernels, shards(): pl.pallas_call(flux_kernel, out_shape=(shape, shape), in_specs=[vmem] * 6...  4.04 us
  transfers between devices with their start and end apart: 4, of which 1 were waited for; matrix products, arithmetic and copies ran while one was open for 1% of the time, Pallas kernels for 0%

profile of v1, /device:TPU:34, one launch (start us, length us, event | category | flops | bytes accessed | tf_op | source)
XLA Modules:
  0.0 152.1 jit_solution(13831593711501799439)
XLA Ops:
  0.6 1.8 %pad_maximum_fusion = f32[32,2,16,512]{3,2,1,0:T(8,128)S(1)} fusion(f32[32,1,16,512]{3,2,1,0:T(8,128)} %bitcast.10, f32[32,1,16,512]{3,2,1,0:T(8,128)} %bitcast.11), kind=kLoop, calls=%fused_computation | loop fusion | flops 524288 | bytes 4194304 | tf_op jit(solution)/shard_map/stack | solution.py:182
  2.4 0.0 copy-start
  2.4 0.0 copy-start.1
  2.5 0.0 copy-start.2
  2.5 0.0 copy-start.3
  2.5 0.0 copy-start.4
  2.5 0.0 copy-start.5
  2.5 61.3 %all_to_all.10.x_ref = f32[32,2,16,512]{3,2,1,0:T(8,128)S(1)} all-to-all(f32[32,2,16,512]{3,2,1,0:T(8,128)S(1)} %pad_maximum_fusion), channel_id=1, replica_groups=mesh['lev'=8,'hor'=32] {'hor'}, dimensions={0} | all-to-all | bytes 4194304 | tf_op jit(solution)/shard_map/all_to_all | solution.py:183
  63.8 0.0 copy-done
  63.8 0.0 copy-done.1
  63.8 0.0 copy-done.2
  63.8 0.0 copy-done.3
  63.8 0.0 copy-done.4
  63.9 0.0 copy-done.5
  63.9 4.8 %spectral.1 = f32[32,2,16,512]{3,2,1,0:T(8,128)S(1)} custom-call(f32[32]{0:T(128)S(1)} %copy-done.3, f32[32]{0:T(128)S(1)} %copy-done.4, f32[32]{0:T(128)S(1)} %copy-done.5, f32[32,2,16,512]{3,2,1,0:T(8,128)S(1)} %all_to_all.10.x_ref, bf16[8,256,256]{2,1,0:T(8,128)(2,1)S(1)} %copy-done, f32[256,2]{1,0:T(8,128)S(1)} %copy-done.1, f32[1,512]{1,0:T(1,128)S(1)} %copy-done.2), custom_call_target="tpu_custom_call" | custom-call | tf_op jit(solution)/shard_map/spectral/pallas_call | solution.py:130
  68.7 45.3 %all_to_all.11.u_ref = f32[32,2,16,512]{3,2,1,0:T(8,128)S(1)} all-to-all(f32[32,2,16,512]{3,2,1,0:T(8,128)S(1)} %spectral.1), channel_id=1, replica_groups=mesh['lev'=8,'hor'=32] {'hor'}, dimensions={0} | all-to-all | bytes 4194304 | tf_op jit(solution)/shard_map/all_to_all | solution.py:185
  114.0 0.0 copy-start.6
  114.0 16.1 %collective-permute-start.1 = (f32[2,16,512]{2,1,0:T(8,128)S(1)}, f32[2,16,512]{2,1,0:T(8,128)S(1)}, u32[]{:S(2)}, u32[]{:S(2)}) collective-permute-start(f32[2,16,512]{2,1,0:T(8,128)S(1)} %get-tuple-element.2), channel_id=1, source_target_pairs={{32,0},{64,32},{96,64},{128,96},{160,128},{192,160},{224,192},{33,... | collective-permute-start | bytes 196616 | tf_op jit(solution)/shard_map/ppermute | solution.py:187
  130.1 1.9 %collective-permute-start = (f32[2,16,512]{2,1,0:T(8,128)S(1)}, f32[2,16,512]{2,1,0:T(8,128)S(1)}, u32[]{:S(2)}, u32[]{:S(2)}) collective-permute-start(f32[2,16,512]{2,1,0:T(8,128)S(1)} %get-tuple-element.3), channel_id=1, source_target_pairs={{0,32},{32,64},{64,96},{96,128},{128,160},{160,192},{192,224},{1,3... | collective-permute-start | bytes 196616 | tf_op jit(solution)/shard_map/ppermute | solution.py:186
  132.0 0.8 slice_bitcast_fusion.2
  132.8 6.0 %collective-permute-start.3 = (f32[16,512]{1,0:T(8,128)S(1)}, f32[16,512]{1,0:T(8,128)S(1)}, u32[]{:S(2)}, u32[]{:S(2)}) collective-permute-start(f32[16,512]{1,0:T(8,128)S(1)} %get-tuple-element.4), channel_id=1, source_target_pairs={{32,0},{64,32},{96,64},{128,96},{160,128},{192,160},{224,192},{33,... | collective-permute-start | bytes 98312 | tf_op jit(solution)/shard_map/ppermute | solution.py:181
  138.9 1.9 %collective-permute-start.2 = (f32[16,512]{1,0:T(8,128)S(1)}, f32[16,512]{1,0:T(8,128)S(1)}, u32[]{:S(2)}, u32[]{:S(2)}) collective-permute-start(f32[16,512]{1,0:T(8,128)S(1)} %get-tuple-element.5), channel_id=1, source_target_pairs={{0,32},{32,64},{64,96},{96,128},{128,160},{160,192},{192,224},{1,3... | collective-permute-start | bytes 98312 | tf_op jit(solution)/shard_map/ppermute | solution.py:180
  140.8 0.0 collective-permute-done.3.whigh_ref
  140.8 0.0 copy-start.9
  140.8 6.0 %collective-permute-done.2.wlow_ref = f32[16,512]{1,0:T(8,128)S(1)} collective-permute-done((f32[16,512]{1,0:T(8,128)S(1)}, f32[16,512]{1,0:T(8,128)S(1)}, u32[]{:S(2)}, u32[]{:S(2)}) %collective-permute-start.2) | collective-permute-done | bytes 32800 | tf_op jit(solution)/shard_map/ppermute | solution.py:180
  146.8 0.0 copy-start.10
  146.8 0.0 collective-permute-done.1.high_ref
  146.8 0.0 copy-start.7
  146.8 0.0 collective-permute-done.low_ref
  146.8 0.0 copy-done.6
  146.8 0.0 copy-done.9
  146.8 0.6 copy-done.10
  147.4 0.0 copy-done.7
  147.4 0.0 copy-start.8
  147.4 0.6 copy-done.8
  148.0 4.0 %flux.1 = (f32[32,16,512]{2,1,0:T(8,128)}, f32[32,16,512]{2,1,0:T(8,128)}) custom-call(f32[32,2,16,512]{3,2,1,0:T(8,128)} %copy-done.6, f32[32,16,512]{2,1,0:T(8,128)} %w_ref.1, f32[2,16,512]{2,1,0:T(8,128)} %copy-done.8, f32[2,16,512]{2,1,0:T(8,128)} %copy-done.7, f32[16,512]{1,0:T(8,128)} %copy-done.10, f32[16,512]{1,0:T(8,128)} %copy-done.9), custom_call_target="tpu_custom_call" | custom-call | tf_op jit(solution)/shard_map/flux/pallas_call | solution.py:190
  (1 shorter events, 0.0 us)
Async XLA Ops:
  2.4 61.4 %copy-start = (bf16[8,256,256]{2,1,0:T(8,128)(2,1)S(1)}, bf16[8,256,256]{2,1,0:T(8,128)(2,1)}, u32[]{:S(2)}) copy-start(bf16[8,256,256]{2,1,0:T(8,128)(2,1)} %constant.6.clone.tab_ref) | copy-start | bytes 3145732
  2.4 61.4 %copy-start.1 = (f32[256,2]{1,0:T(8,128)S(1)}, f32[256,2]{1,0:T(8,128)}, u32[]{:S(2)}) copy-start(f32[256,2]{1,0:T(8,128)} %constant.7.clone.sq_ref) | copy-start | bytes 6148
  2.5 61.4 %copy-start.2 = (f32[1,512]{1,0:T(1,128)S(1)}, f32[1,512]{1,0:T(1,128)}, u32[]{:S(2)}) copy-start(f32[1,512]{1,0:T(1,128)} %constant.8.clone.sqt_ref) | copy-start | bytes 6148
  2.5 61.4 %copy-start.3 = (f32[32]{0:T(128)S(1)}, f32[32]{0:T(128)}, u32[]{:S(2)}) copy-start(f32[32]{0:T(128)} %rt_ref.1) | copy-start | bytes 388
  2.5 61.4 %copy-start.4 = (f32[32]{0:T(128)S(1)}, f32[32]{0:T(128)}, u32[]{:S(2)}) copy-start(f32[32]{0:T(128)} %rs_ref.1) | copy-start | bytes 388
  2.5 61.4 %copy-start.5 = (f32[32]{0:T(128)S(1)}, f32[32]{0:T(128)}, u32[]{:S(2)}) copy-start(f32[32]{0:T(128)} %rc_ref.1) | copy-start | bytes 388
  114.0 32.8 %copy-start.6 = (f32[32,2,16,512]{3,2,1,0:T(8,128)}, f32[32,2,16,512]{3,2,1,0:T(8,128)S(1)}, u32[]{:S(2)}) copy-start(f32[32,2,16,512]{3,2,1,0:T(8,128)S(1)} %all_to_all.11.u_ref) | copy-start | bytes 6291460
  114.0 32.8 %collective-permute-start.1 = (f32[2,16,512]{2,1,0:T(8,128)S(1)}, f32[2,16,512]{2,1,0:T(8,128)S(1)}, u32[]{:S(2)}, u32[]{:S(2)}) collective-permute-start(f32[2,16,512]{2,1,0:T(8,128)S(1)} %get-tuple-element.2), channel_id=1, source_target_pairs={{32,0},{64,32},{96,64},{128,96},{160,128},{192,160},{224,192},{33,... | collective-permute-start | bytes 196616 | tf_op jit(solution)/shard_map/ppermute | solution.py:187
  130.1 16.7 %collective-permute-start = (f32[2,16,512]{2,1,0:T(8,128)S(1)}, f32[2,16,512]{2,1,0:T(8,128)S(1)}, u32[]{:S(2)}, u32[]{:S(2)}) collective-permute-start(f32[2,16,512]{2,1,0:T(8,128)S(1)} %get-tuple-element.3), channel_id=1, source_target_pairs={{0,32},{32,64},{64,96},{96,128},{128,160},{160,192},{192,224},{1,3... | collective-permute-start | bytes 196616 | tf_op jit(solution)/shard_map/ppermute | solution.py:186
  132.8 8.0 %collective-permute-start.3 = (f32[16,512]{1,0:T(8,128)S(1)}, f32[16,512]{1,0:T(8,128)S(1)}, u32[]{:S(2)}, u32[]{:S(2)}) collective-permute-start(f32[16,512]{1,0:T(8,128)S(1)} %get-tuple-element.4), channel_id=1, source_target_pairs={{32,0},{64,32},{96,64},{128,96},{160,128},{192,160},{224,192},{33,... | collective-permute-start | bytes 98312 | tf_op jit(solution)/shard_map/ppermute | solution.py:181
  138.9 7.9 %collective-permute-start.2 = (f32[16,512]{1,0:T(8,128)S(1)}, f32[16,512]{1,0:T(8,128)S(1)}, u32[]{:S(2)}, u32[]{:S(2)}) collective-permute-start(f32[16,512]{1,0:T(8,128)S(1)} %get-tuple-element.5), channel_id=1, source_target_pairs={{0,32},{32,64},{64,96},{96,128},{128,160},{160,192},{192,224},{1,3... | collective-permute-start | bytes 98312 | tf_op jit(solution)/shard_map/ppermute | solution.py:180
  140.8 6.0 %copy-start.9 = (f32[16,512]{1,0:T(8,128)}, f32[16,512]{1,0:T(8,128)S(1)}, u32[]{:S(2)}) copy-start(f32[16,512]{1,0:T(8,128)S(1)} %collective-permute-done.3.whigh_ref) | copy-start | bytes 98308
  146.8 0.6 copy-start.10
  146.8 0.6 copy-start.7
  147.4 0.6 copy-start.8

commit v2 on v1

v2 whole, which is shorter than its diff:
```python
import functools
import math

import jax
import jax.numpy as jnp
import numpy as np
from jax import lax
from jax.experimental import pallas as pl
from jax.experimental.pallas import tpu as pltpu
from jax.sharding import PartitionSpec as P


buoyancy = 0.5
advective_number = 0.25


def real_basis(length):
    half = length // 2
    points = np.arange(half)
    tables, waves = [], []
    for parity in (0, 1):
        cos_waves = np.arange(parity, half + 1, 2)
        sin_waves = np.array([k for k in cos_waves if 0 < k < half])
        rows = []
        for k in cos_waves:
            weight = math.sqrt((1.0 if k in (0, half) else 2.0) / length)
            rows.append(weight * np.cos(2.0 * math.pi / length * ((k * points) % length)))
        for k in sin_waves:
            rows.append(math.sqrt(2.0 / length) * np.sin(2.0 * math.pi / length * ((k * points) % length)))
        tables.append(np.stack(rows))
        waves.append(np.concatenate([cos_waves, sin_waves]))
    return tables, waves


def parts_of(table):
    kind = np.dtype(jnp.bfloat16)
    high = table.astype(kind)
    return high, (table - high.astype(np.float64)).astype(kind)


def split(value):
    high = value.astype(jnp.bfloat16)
    low = (value - high.astype(jnp.float32)).astype(jnp.bfloat16)
    return high, low


def dot(left, right):
    return jnp.dot(left, right, preferred_element_type=jnp.float32)


def right_product(value, table_high, table_low):
    high, low = split(value)
    return dot(high, table_high) + dot(low, table_high) + dot(high, table_low)


def left_product(table_high, table_low, value):
    high, low = split(value)
    return dot(table_high, high) + dot(table_low, high) + dot(table_high, low)


def position():
    at = lax.axis_index("hor")
    return at // 8, (at // 2) % 4, at % 2


def block_to(place, step, near):
    z, x, c = place
    return ((z + step) % 4) * 8 + ((x + near // 2) % 4) * 2 + (c + near % 2) % 2


def block_from(place, step, near):
    z, x, c = place
    return ((z + 4 - step) % 4) * 8 + ((x + 4 - near // 2) % 4) * 2 + (c + near % 2) % 2


def fold_kernel(heat_ref, salt_ref, *refs):
    half = heat_ref.shape[-1] // 2
    by_step, by_near = refs[:4], refs[4:]
    place = position()
    for step in range(4):
        for near in range(8):
            level = block_to(place, step, near)
            for f, ref in enumerate((heat_ref, salt_ref)):
                value = ref[level]
                by_step[step][near, f] = value[:, :half] + value[:, half:]
                by_near[near][step, f] = value[:, :half] - value[:, half:]


def repack_kernel(*refs):
    groups = 32 // refs[0].shape[0]
    for i in range(groups):
        for j in range(32 // groups):
            refs[groups + j][i] = refs[i][j]


def gathered(refs, out_ref):
    place = position()
    for i, ref in enumerate(refs):
        for j in range(ref.shape[0]):
            step, near = (i, j) if len(refs) == 4 else (j, i)
            out_ref[block_from(place, step, near)] = ref[j]


def unpack_kernel(*refs):
    pieces, (out_ref, first_ref, last_ref) = refs[:-3], refs[-3:]
    gathered(pieces, out_ref)
    first_ref[...] = out_ref[0]
    last_ref[...] = out_ref[out_ref.shape[0] - 1]


def transformed(parity, rates, x_ref, tab_ref, sq_ref, sqt_ref):
    half = x_ref.shape[-1]
    length = 2 * half
    rate_t, rate_s, rate_c = rates

    def table(which, transposed, low):
        return tab_ref[which * 4 + transposed * 2 + low]

    planes = []
    for f in (0, 1):
        value = x_ref[:, f].reshape(length, half)
        planes += [value[:half] + value[half:], value[:half] - value[half:]]
    inner = right_product(
        jnp.concatenate(planes, axis=0), table(parity, 1, 0), table(parity, 1, 1)
    )
    back = {}
    for p in (0, 1):
        stacked = jnp.concatenate(
            [inner[(2 * f + p) * half : (2 * f + p + 1) * half] for f in (0, 1)], axis=1
        )
        product = left_product(table(p, 0, 0), table(p, 0, 1), stacked)
        temp, salt = product[:, :half], product[:, half:]
        modulus = (sq_ref[:, p : p + 1] + sqt_ref[parity : parity + 1]) / (
            (length / 2.0) * (length / 2.0)
        )
        diag_temp = 1.0 + rate_t * modulus
        diag_salt = 1.0 + rate_s * modulus
        cross = rate_c * modulus
        determinant = diag_temp * diag_salt + cross * cross
        new_temp = (diag_salt * temp - cross * salt) / determinant
        new_salt = (diag_temp * salt + cross * temp) / determinant
        product = left_product(
            table(p, 1, 0), table(p, 1, 1), jnp.concatenate([new_temp, new_salt], axis=1)
        )
        for f in (0, 1):
            back[f, p] = product[:, f * half : (f + 1) * half]
    stacked = jnp.concatenate([back[f, p] for f in (0, 1) for p in (0, 1)], axis=0)
    result = right_product(stacked, table(parity, 0, 0), table(parity, 0, 1))
    out = []
    for f in (0, 1):
        plus = result[2 * f * half : (2 * f + 1) * half]
        minus = result[(2 * f + 1) * half : (2 * f + 2) * half]
        out.append((plus + minus, plus - minus))
    return out


def store_rows(out_ref, result):
    blocks, _, rows, half = out_ref.shape
    for f in (0, 1):
        for side in (0, 1):
            at = slice(side * blocks // 2, (side + 1) * blocks // 2)
            out_ref[at, f] = result[f][side].reshape(blocks // 2, rows, half)


def spectral_kernel(parity, rt_ref, rs_ref, rc_ref, tab_ref, sq_ref, sqt_ref, *refs):
    inputs, outs, held = (refs[:8], refs[8:12], refs[12]) if parity == 0 else (refs[:4], refs[4:12], refs[12])
    gathered(inputs, held)
    level = lax.axis_index("hor")
    rates = (rt_ref[level], rs_ref[level], rc_ref[level])
    store_rows(held, transformed(parity, rates, held, tab_ref, sq_ref, sqt_ref))
    place = position()
    for step in range(4):
        for near in range(8):
            block = held[block_to(place, step, near)]
            if parity == 0:
                outs[step][near] = block
            else:
                outs[near][step] = block


def flux_kernel(
    even_ref, odd_ref, w_ref, elow_ref, ehigh_ref, olow_ref, ohigh_ref, wlow_ref, whigh_ref, t_out, s_out
):
    levels = w_ref.shape[0]
    block = lax.axis_index("lev")
    last = lax.axis_size("lev") - 1

    def unfolded(even, odd):
        return tuple(
            jnp.concatenate([even[f] + odd[f], even[f] - odd[f]], axis=-1) for f in (0, 1)
        )

    def at_level(level):
        return unfolded(even_ref[level], odd_ref[level]) + (w_ref[level],)

    def face(lower, upper):
        lt, ls, lw = lower
        ut, us, uw = upper
        flow = 0.5 * (lw + uw) + buoyancy * 0.5 * ((lt + ut) - (ls + us))
        up = jnp.maximum(flow, 0.0)
        down = jnp.minimum(flow, 0.0)
        return up * lt + down * ut, up * ls + down * us

    at = at_level(0)
    below = face(unfolded(elow_ref[...], olow_ref[...]) + (wlow_ref[...],), at)
    below = tuple(jnp.where(block > 0, b, 0.0) for b in below)
    for level in range(levels):
        if level + 1 < levels:
            nxt = at_level(level + 1)
            above = face(at, nxt)
        else:
            nxt = unfolded(ehigh_ref[...], ohigh_ref[...]) + (whigh_ref[...],)
            above = tuple(jnp.where(block < last, a, 0.0) for a in face(at, nxt))
        t_out[level] = at[0] - advective_number * (above[0] - below[0])
        s_out[level] = at[1] - advective_number * (above[1] - below[1])
        at, below = nxt, above


def constants(length):
    tables, waves = real_basis(length)
    stack = []
    for table in tables:
        for oriented in (table, table.T):
            stack.extend(parts_of(oriented))
    squares = np.stack([w.astype(np.float32) ** 2 for w in waves], axis=1)
    return np.stack(stack), squares, np.ascontiguousarray(squares.T)


vmem = pl.BlockSpec(memory_space=pltpu.VMEM)
smem = pl.BlockSpec(memory_space=pltpu.SMEM)


def call(kernel, outs, *args, smem_args=0, scratch=(), flops=0):
    moved = sum(math.prod(a.shape) * 4 for a in args) + sum(math.prod(o.shape) * 4 for o in outs)
    return pl.pallas_call(
        kernel,
        out_shape=tuple(outs),
        in_specs=[smem] * smem_args + [vmem] * (len(args) - smem_args),
        out_specs=(vmem,) * len(outs),
        scratch_shapes=scratch,
        compiler_params=pltpu.CompilerParams(vmem_limit_bytes=24 << 20),
        cost_estimate=pl.CostEstimate(flops=flops, bytes_accessed=moved, transcendentals=0),
    )(*args)


def step_of(heat, saline, updraft, rate_t, rate_s, rate_c):
    levels, rows, length = heat.shape
    half = length // 2
    f32 = jnp.float32
    by_plane = jax.ShapeDtypeStruct((8, 2, rows, half), f32)
    by_near = jax.ShapeDtypeStruct((4, 2, rows, half), f32)
    whole = jax.ShapeDtypeStruct((levels, 2, rows, half), f32)
    edge = jax.ShapeDtypeStruct((2, rows, half), f32)
    table, squares, squares_t = (jnp.asarray(c) for c in constants(length))
    shared = (rate_t, rate_s, rate_c, table, squares, squares_t)
    flops = 3 * 16 * 2 * half**3

    def along_z(pieces):
        out = [pieces[0]]
        for step in (1, 2, 3):
            pairs = [(h, (h + 8 * step) % 32) for h in range(32)]
            out.append(lax.ppermute(pieces[step], "hor", pairs))
        return out

    def in_plane(pieces):
        out = [pieces[0]]
        for near in range(1, 8):
            pairs = [
                (z * 8 + x * 2 + c, z * 8 + (x + near // 2) % 4 * 2 + (c + near) % 2)
                for z in range(4)
                for x in range(4)
                for c in range(2)
            ]
            out.append(lax.ppermute(pieces[near], "hor", pairs))
        return out

    def halo(first, last):
        return lax.ppermute(last, "lev", upward), lax.ppermute(first, "lev", downward)

    def kernel(body, outs, *args, **kwargs):
        return call(body, outs, *args, **kwargs)

    def repacked(pieces):
        outs = [by_near] * 8 if len(pieces) == 4 else [by_plane] * 4
        return kernel(repack_kernel, outs, *pieces)

    def solved(parity, pieces):
        outs = [by_plane] * 4 if parity == 0 else [by_near] * 8
        return kernel(
            functools.partial(spectral_kernel, parity), outs, *shared, *pieces,
            smem_args=3, flops=flops, scratch=[pltpu.VMEM(whole.shape, f32)],
        )

    count = lax.axis_size("lev")
    upward = [(i, i + 1) for i in range(count - 1)]
    downward = [(i + 1, i) for i in range(count - 1)]

    folded = kernel(fold_kernel, [by_plane] * 4 + [by_near] * 8, heat, saline)
    even, odd = folded[:4], folded[4:]
    even = along_z(even)
    odd = in_plane(odd)
    w_halo = halo(updraft[0], updraft[-1])
    odd = along_z(repacked(odd))
    even = in_plane(repacked(even))
    even = along_z(solved(0, even))
    odd = in_plane(solved(1, odd))
    odd = along_z(repacked(odd))
    even = in_plane(repacked(even))
    even, *even_ends = kernel(unpack_kernel, [whole, edge, edge], *even)
    even_halo = halo(*even_ends)
    odd, *odd_ends = kernel(unpack_kernel, [whole, edge, edge], *odd)
    odd_halo = halo(*odd_ends)
    field = jax.ShapeDtypeStruct(heat.shape, f32)
    return kernel(flux_kernel, [field, field], even, odd, updraft, *even_halo, *odd_halo, *w_halo)


def solution(mesh):
    field = P("lev", "hor", None)
    return jax.shard_map(
        step_of,
        mesh=mesh,
        in_specs=(field,) * 3 + (P("lev"),) * 3,
        out_specs=(field, field),
        check_vma=False,
    )
```

time: 152 us -> 182 us (1.20)
  the two profiles are of different devices: /device:TPU:34 before, /device:TPU:24 now
where the time goes in v2:
time: 182 us
  starting transfers between devices  84.4 us (46%)
  waiting for transfers between devices  83.9 us (46%)
  Pallas kernels  10.1 us (6%)
  local copies, waits for them, and re-layouts  2.47 us (1%)
    ppermute x12, waiting for transfers between devices, along_z(): out.append(lax.ppermute(pieces[step], 'hor', pairs))  62.5 us
    ppermute x12, starting transfers between devices, along_z(): out.append(lax.ppermute(pieces[step], 'hor', pairs))  33.5 us
    ppermute x28, starting transfers between devices, in_plane(): out.append(lax.ppermute(pieces[near], 'hor', pairs))  31.2 us
    ppermute x28, waiting for transfers between devices, in_plane(): out.append(lax.ppermute(pieces[near], 'hor', pairs))  15.5 us
    ppermute x3, starting transfers between devices, halo(): lax.ppermute(last, 'lev', upward)  11.3 us
    pallas_call x10, Pallas kernels, call(): pl.pallas_call(kernel, out_shape=tuple(outs), in_specs=[smem] * smem_args...  10.1 us
    ppermute x3, starting transfers between devices, halo(): lax.ppermute(first, 'lev', downward)  8.48 us
    ppermute x3, waiting for transfers between devices, halo(): lax.ppermute(first, 'lev', downward)  5.95 us
  transfers between devices with their start and end apart: 46, of which 13 were waited for; matrix products, arithmetic and copies ran while one was open for 0% of the time, Pallas kernels for 4%

profile of v2, /device:TPU:24, one launch (start us, length us, event | category | flops | bytes accessed | tf_op | source)
XLA Modules:
  0.0 181.9 jit_solution(3364423609081863137)
XLA Ops:
  0.6 1.2 copy-done.1
  1.9 1.2 copy-done.2
  3.1 0.1 shard_map.104
  3.2 0.1 collective-permute-start.20
  3.3 1.6 collective-permute-start.21
  4.9 1.2 collective-permute-start.22
  6.1 1.7 collective-permute-start.23
  7.8 1.5 collective-permute-start.24
  9.4 3.3 %collective-permute-start = (f32[8,2,16,256]{3,2,1,0:T(8,128)S(1)}, f32[8,2,16,256]{3,2,1,0:T(8,128)S(1)}, u32[]{:S(2)}, u32[]{:S(2)}) collective-permute-start(f32[8,2,16,256]{3,2,1,0:T(8,128)S(1)} %get-tuple-element.57), channel_id=1, source_target_pairs={{0,8},{1,9},{2,10},{3,11},{4,12},{5,13},{6,14},{7,15},{8,16},{9,17... | collective-permute-start | bytes 786440 | tf_op jit(solution)/shard_map/ppermute | solution.py:262
  12.6 1.7 collective-permute-start.25
  14.4 0.7 collective-permute-start.26
  15.1 2.5 %collective-permute-done.23.refs_4_ = f32[4,2,16,256]{3,2,1,0:T(8,128)S(1)} collective-permute-done((f32[4,2,16,256]{3,2,1,0:T(8,128)S(1)}, f32[4,2,16,256]{3,2,1,0:T(8,128)S(1)}, u32[]{:S(2)}, u32[]{:S(2)}) %collective-permute-start.23) | collective-permute-done | bytes 131104 | tf_op jit(solution)/shard_map/ppermute | solution.py:274
  17.6 7.2 %collective-permute-start.1 = (f32[8,2,16,256]{3,2,1,0:T(8,128)S(1)}, f32[8,2,16,256]{3,2,1,0:T(8,128)S(1)}, u32[]{:S(2)}, u32[]{:S(2)}) collective-permute-start(f32[8,2,16,256]{3,2,1,0:T(8,128)S(1)} %get-tuple-element.58), channel_id=1, source_target_pairs={{0,16},{1,17},{2,18},{3,19},{4,20},{5,21},{6,22},{7,23},{8,24},{9,... | collective-permute-start | bytes 786440 | tf_op jit(solution)/shard_map/ppermute | solution.py:262
  24.8 0.8 collective-permute-start.2
  25.6 0.1 shard_map.109
  25.7 2.2 %collective-permute-start.27 = (f32[8,2,16,256]{3,2,1,0:T(8,128)S(1)}, f32[8,2,16,256]{3,2,1,0:T(8,128)S(1)}, u32[]{:S(2)}, u32[]{:S(2)}) collective-permute-start(f32[8,2,16,256]{3,2,1,0:T(8,128)S(1)} %get-tuple-element.90), channel_id=1, source_target_pairs={{0,8},{1,9},{2,10},{3,11},{4,12},{5,13},{6,14},{7,15},{8,16},{9,17... | collective-permute-start | bytes 786440 | tf_op jit(solution)/shard_map/ppermute | solution.py:262
  27.9 2.2 %collective-permute-start.28 = (f32[8,2,16,256]{3,2,1,0:T(8,128)S(1)}, f32[8,2,16,256]{3,2,1,0:T(8,128)S(1)}, u32[]{:S(2)}, u32[]{:S(2)}) collective-permute-start(f32[8,2,16,256]{3,2,1,0:T(8,128)S(1)} %get-tuple-element.91), channel_id=1, source_target_pairs={{0,16},{1,17},{2,18},{3,19},{4,20},{5,21},{6,22},{7,23},{8,24},{9,... | collective-permute-start | bytes 786440 | tf_op jit(solution)/shard_map/ppermute | solution.py:262
  30.1 4.0 %collective-permute-start.29 = (f32[8,2,16,256]{3,2,1,0:T(8,128)S(1)}, f32[8,2,16,256]{3,2,1,0:T(8,128)S(1)}, u32[]{:S(2)}, u32[]{:S(2)}) collective-permute-start(f32[8,2,16,256]{3,2,1,0:T(8,128)S(1)} %get-tuple-element.92), channel_id=1, source_target_pairs={{0,24},{1,25},{2,26},{3,27},{4,28},{5,29},{6,30},{7,31},{8,0},{9,1... | collective-permute-start | bytes 786440 | tf_op jit(solution)/shard_map/ppermute | solution.py:262
  34.1 6.9 %collective-permute-done.1.refs_2_ = f32[8,2,16,256]{3,2,1,0:T(8,128)S(1)} collective-permute-done((f32[8,2,16,256]{3,2,1,0:T(8,128)S(1)}, f32[8,2,16,256]{3,2,1,0:T(8,128)S(1)}, u32[]{:S(2)}, u32[]{:S(2)}) %collective-permute-start.1) | collective-permute-done | bytes 262176 | tf_op jit(solution)/shard_map/ppermute | solution.py:262
  41.1 23.5 %collective-permute-done.2.refs_3_ = f32[8,2,16,256]{3,2,1,0:T(8,128)S(1)} collective-permute-done((f32[8,2,16,256]{3,2,1,0:T(8,128)S(1)}, f32[8,2,16,256]{3,2,1,0:T(8,128)S(1)}, u32[]{:S(2)}, u32[]{:S(2)}) %collective-permute-start.2) | collective-permute-done | bytes 262176 | tf_op jit(solution)/shard_map/ppermute | solution.py:262
  64.7 0.1 collective-permute-start.3
  64.8 0.1 collective-permute-start.4
  64.9 0.5 collective-permute-start.5
  65.3 3.9 %collective-permute-start.6 = (f32[4,2,16,256]{3,2,1,0:T(8,128)S(1)}, f32[4,2,16,256]{3,2,1,0:T(8,128)S(1)}, u32[]{:S(2)}, u32[]{:S(2)}) collective-permute-start(f32[4,2,16,256]{3,2,1,0:T(8,128)S(1)} %get-tuple-element.64), channel_id=1, source_target_pairs={{0,4},{1,5},{2,6},{3,7},{4,0},{5,1},{6,2},{7,3},{8,12},{9,13},{10,... | collective-permute-start | bytes 393224 | tf_op jit(solution)/shard_map/ppermute | solution.py:274
  69.3 0.8 collective-permute-done.29.refs_3_
  70.1 0.4 collective-permute-start.7
  70.5 1.2 collective-permute-start.8
  71.7 0.7 collective-permute-done.4.refs_2_
  72.4 1.3 collective-permute-start.9
  73.8 3.7 %shard_map.110 = (f32[4,2,16,256]{3,2,1,0:T(8,128)S(1)}, f32[4,2,16,256]{3,2,1,0:T(8,128)S(1)}, f32[4,2,16,256]{3,2,1,0:T(8,128)S(1)}, f32[4,2,16,256]{3,2,1,0:T...) custom-call(f32[32]{0:T(128)S(1)} %copy-done.3, ...), custom_call_target="tpu_custom_call" | custom-call | flops 1610612736 | bytes 4198784 | tf_op jit(solution)/shard_map/pallas_call | solution.py:235
  77.5 2.3 %collective-permute-done.5.refs_3_ = f32[4,2,16,256]{3,2,1,0:T(8,128)S(1)} collective-permute-done((f32[4,2,16,256]{3,2,1,0:T(8,128)S(1)}, f32[4,2,16,256]{3,2,1,0:T(8,128)S(1)}, u32[]{:S(2)}, u32[]{:S(2)}) %collective-permute-start.5) | collective-permute-done | bytes 131104 | tf_op jit(solution)/shard_map/ppermute | solution.py:274
  79.7 0.4 collective-permute-start.30
  80.1 0.1 collective-permute-start.32
  80.2 4.1 %collective-permute-start.33 = (f32[4,2,16,256]{3,2,1,0:T(8,128)S(1)}, f32[4,2,16,256]{3,2,1,0:T(8,128)S(1)}, u32[]{:S(2)}, u32[]{:S(2)}) collective-permute-start(f32[4,2,16,256]{3,2,1,0:T(8,128)S(1)} %get-tuple-element.97), channel_id=1, source_target_pairs={{0,4},{1,5},{2,6},{3,7},{4,0},{5,1},{6,2},{7,3},{8,12},{9,13},{10,... | collective-permute-start | bytes 393224 | tf_op jit(solution)/shard_map/ppermute | solution.py:274
  84.3 0.4 collective-permute-start.34
  84.6 3.7 %shard_map.106 = (f32[8,2,16,256]{3,2,1,0:T(8,128)S(1)}, f32[8,2,16,256]{3,2,1,0:T(8,128)S(1)}, f32[8,2,16,256]{3,2,1,0:T(8,128)S(1)}, f32[8,2,16,256]{3,2,1,0:T(8,128)S(1)}) custom-call(f32[32]{0:T(128)S(1)} %copy-done.3, f32[32]{0:T(128)S(1)} %copy-done.4, f32[32]{0:T(128)S(1)} %copy-done.5, bf16[8,256,256]{2,1,0:T(8,128)(2,1)S(1)} %copy-done.6, ...), custom_call_target="tpu_custom_call" | custom-call | flops 1610612736 | bytes 4198784 | tf_op jit(solution)/shard_map/pallas_call | solution.py:235
  88.3 0.6 collective-permute-start.10
  89.0 1.8 collective-permute-start.35
  90.7 3.7 %collective-permute-done.32.refs_3_ = f32[4,2,16,256]{3,2,1,0:T(8,128)S(1)} collective-permute-done((f32[4,2,16,256]{3,2,1,0:T(8,128)S(1)}, f32[4,2,16,256]{3,2,1,0:T(8,128)S(1)}, u32[]{:S(2)}, u32[]{:S(2)}) %collective-permute-start.32) | collective-permute-done | bytes 131104 | tf_op jit(solution)/shard_map/ppermute | solution.py:274
  94.5 2.8 %collective-permute-start.11 = (f32[8,2,16,256]{3,2,1,0:T(8,128)S(1)}, f32[8,2,16,256]{3,2,1,0:T(8,128)S(1)}, u32[]{:S(2)}, u32[]{:S(2)}) collective-permute-start(f32[8,2,16,256]{3,2,1,0:T(8,128)S(1)} %get-tuple-element.70), channel_id=1, source_target_pairs={{0,16},{1,17},{2,18},{3,19},{4,20},{5,21},{6,22},{7,23},{8,24},{9,... | collective-permute-start | bytes 786440 | tf_op jit(solution)/shard_map/ppermute | solution.py:262
  97.2 1.4 collective-permute-start.12
  98.6 0.5 collective-permute-done.36.refs_7_
  99.2 1.4 collective-permute-start.37
  100.6 4.8 %collective-permute-start.38 = (f32[8,2,16,256]{3,2,1,0:T(8,128)S(1)}, f32[8,2,16,256]{3,2,1,0:T(8,128)S(1)}, u32[]{:S(2)}, u32[]{:S(2)}) collective-permute-start(f32[8,2,16,256]{3,2,1,0:T(8,128)S(1)} %get-tuple-element.103), channel_id=1, source_target_pairs={{0,16},{1,17},{2,18},{3,19},{4,20},{5,21},{6,22},{7,23},{8,24},{9,... | collective-permute-start | bytes 786440 | tf_op jit(solution)/shard_map/ppermute | solution.py:262
  105.3 2.9 %collective-permute-start.39 = (f32[8,2,16,256]{3,2,1,0:T(8,128)S(1)}, f32[8,2,16,256]{3,2,1,0:T(8,128)S(1)}, u32[]{:S(2)}, u32[]{:S(2)}) collective-permute-start(f32[8,2,16,256]{3,2,1,0:T(8,128)S(1)} %get-tuple-element.104), channel_id=1, source_target_pairs={{0,24},{1,25},{2,26},{3,27},{4,28},{5,29},{6,30},{7,31},{8,0},{9,1... | collective-permute-start | bytes 786440 | tf_op jit(solution)/shard_map/ppermute | solution.py:262
  108.3 10.7 %collective-permute-done.11.refs_2_ = f32[8,2,16,256]{3,2,1,0:T(8,128)S(1)} collective-permute-done((f32[8,2,16,256]{3,2,1,0:T(8,128)S(1)}, f32[8,2,16,256]{3,2,1,0:T(8,128)S(1)}, u32[]{:S(2)}, u32[]{:S(2)}) %collective-permute-start.11) | collective-permute-done | bytes 262176 | tf_op jit(solution)/shard_map/ppermute | solution.py:262
  118.9 19.6 %collective-permute-done.12.refs_3_ = f32[8,2,16,256]{3,2,1,0:T(8,128)S(1)} collective-permute-done((f32[8,2,16,256]{3,2,1,0:T(8,128)S(1)}, f32[8,2,16,256]{3,2,1,0:T(8,128)S(1)}, u32[]{:S(2)}, u32[]{:S(2)}) %collective-permute-start.12) | collective-permute-done | bytes 262176 | tf_op jit(solution)/shard_map/ppermute | solution.py:262
  138.6 0.2 collective-permute-start.13
  138.8 1.5 collective-permute-start.14
  140.3 2.9 %collective-permute-start.16 = (f32[4,2,16,256]{3,2,1,0:T(8,128)S(1)}, f32[4,2,16,256]{3,2,1,0:T(8,128)S(1)}, u32[]{:S(2)}, u32[]{:S(2)}) collective-permute-start(f32[4,2,16,256]{3,2,1,0:T(8,128)S(1)} %get-tuple-element.76), channel_id=1, source_target_pairs={{0,4},{1,5},{2,6},{3,7},{4,0},{5,1},{6,2},{7,3},{8,12},{9,13},{10,... | collective-permute-start | bytes 393224 | tf_op jit(solution)/shard_map/ppermute | solution.py:274
  143.2 0.9 collective-permute-done.39.refs_3_
  144.2 3.7 %collective-permute-start.18 = (f32[4,2,16,256]{3,2,1,0:T(8,128)S(1)}, f32[4,2,16,256]{3,2,1,0:T(8,128)S(1)}, u32[]{:S(2)}, u32[]{:S(2)}) collective-permute-start(f32[4,2,16,256]{3,2,1,0:T(8,128)S(1)} %get-tuple-element.78), channel_id=1, source_target_pairs={{0,6},{1,7},{2,0},{3,1},{4,2},{5,3},{6,4},{7,5},{8,14},{9,15},{10,... | collective-permute-start | bytes 393224 | tf_op jit(solution)/shard_map/ppermute | solution.py:274
  147.8 0.2 collective-permute-start.19
  148.0 5.7 %collective-permute-done.15.refs_3_ = f32[4,2,16,256]{3,2,1,0:T(8,128)S(1)} collective-permute-done((f32[4,2,16,256]{3,2,1,0:T(8,128)S(1)}, f32[4,2,16,256]{3,2,1,0:T(8,128)S(1)}, u32[]{:S(2)}, u32[]{:S(2)}) %collective-permute-start.15) | collective-permute-done | bytes 131104 | tf_op jit(solution)/shard_map/ppermute | solution.py:274
  153.7 2.6 %collective-permute-start.45 = (f32[16,512]{1,0:T(8,128)S(1)}, f32[16,512]{1,0:T(8,128)S(1)}, u32[]{:S(2)}, u32[]{:S(2)}) collective-permute-start(f32[16,512]{1,0:T(8,128)S(1)} %get-tuple-element.110), channel_id=1, source_target_pairs={{32,0},{64,32},{96,64},{128,96},{160,128},{192,160},{224,192},{33,... | collective-permute-start | bytes 98312 | tf_op jit(solution)/shard_map/ppermute | solution.py:278
  156.3 0.1 shard_map.112
  156.5 5.3 %collective-permute-start.44 = (f32[16,512]{1,0:T(8,128)S(1)}, f32[16,512]{1,0:T(8,128)S(1)}, u32[]{:S(2)}, u32[]{:S(2)}) collective-permute-start(f32[16,512]{1,0:T(8,128)S(1)} %get-tuple-element.111), channel_id=1, source_target_pairs={{0,32},{32,64},{64,96},{96,128},{128,160},{160,192},{192,224},{1,3... | collective-permute-start | bytes 98312 | tf_op jit(solution)/shard_map/ppermute | solution.py:278
  161.8 1.9 %collective-permute-start.42 = (f32[2,16,256]{2,1,0:T(8,128)S(1)}, f32[2,16,256]{2,1,0:T(8,128)S(1)}, u32[]{:S(2)}, u32[]{:S(2)}) collective-permute-start(f32[2,16,256]{2,1,0:T(8,128)S(1)} %get-tuple-element.108), channel_id=1, source_target_pairs={{0,32},{32,64},{64,96},{96,128},{128,160},{160,192},{192,224},{1,3... | collective-permute-start | bytes 98312 | tf_op jit(solution)/shard_map/ppermute | solution.py:278
  163.7 3.9 %collective-permute-start.43 = (f32[2,16,256]{2,1,0:T(8,128)S(1)}, f32[2,16,256]{2,1,0:T(8,128)S(1)}, u32[]{:S(2)}, u32[]{:S(2)}) collective-permute-start(f32[2,16,256]{2,1,0:T(8,128)S(1)} %get-tuple-element.109), channel_id=1, source_target_pairs={{32,0},{64,32},{96,64},{128,96},{160,128},{192,160},{224,192},{33,... | collective-permute-start | bytes 98312 | tf_op jit(solution)/shard_map/ppermute | solution.py:278
  167.7 0.1 shard_map.108
  167.8 4.0 %collective-permute-start.40 = (f32[2,16,256]{2,1,0:T(8,128)S(1)}, f32[2,16,256]{2,1,0:T(8,128)S(1)}, u32[]{:S(2)}, u32[]{:S(2)}) collective-permute-start(f32[2,16,256]{2,1,0:T(8,128)S(1)} %get-tuple-element.106), channel_id=1, source_target_pairs={{0,32},{32,64},{64,96},{96,128},{128,160},{160,192},{192,224},{1,3... | collective-permute-start | bytes 98312 | tf_op jit(solution)/shard_map/ppermute | solution.py:278
  171.8 1.9 %collective-permute-start.41 = (f32[2,16,256]{2,1,0:T(8,128)S(1)}, f32[2,16,256]{2,1,0:T(8,128)S(1)}, u32[]{:S(2)}, u32[]{:S(2)}) collective-permute-start(f32[2,16,256]{2,1,0:T(8,128)S(1)} %get-tuple-element.107), channel_id=1, source_target_pairs={{32,0},{64,32},{96,64},{128,96},{160,128},{192,160},{224,192},{33,... | collective-permute-start | bytes 98312 | tf_op jit(solution)/shard_map/ppermute | solution.py:278
  173.8 5.9 %collective-permute-done.41.ehigh_ref = f32[2,16,256]{2,1,0:T(8,128)S(1)} collective-permute-done((f32[2,16,256]{2,1,0:T(8,128)S(1)}, f32[2,16,256]{2,1,0:T(8,128)S(1)}, u32[]{:S(2)}, u32[]{:S(2)}) %collective-permute-start.41) | collective-permute-done | bytes 32800 | tf_op jit(solution)/shard_map/ppermute | solution.py:278
  179.7 2.2 %shard_map.113 = (f32[32,16,512]{2,1,0:T(8,128)}, f32[32,16,512]{2,1,0:T(8,128)}) custom-call(f32[32,2,16,256]{3,2,1,0:T(8,128)S(1)} %get-tuple-element.80.even_ref, f32[32,2,16,256]{3,2,1,0:T(8,128)S(1)} %get-tuple-element.105.odd_ref, f32[32,16,512]{2,1,0:T(8,128)S(1)} %copy-done, f32[2,16,256]{2,1,0:T(8,128)S(1)} %collective-permute-done.40.elow_ref, ...), custom_call_target="tpu_custom_call" | custom-call | bytes 5439488 | tf_op jit(solution)/shard_map/pallas_call | solution.py:235
  (57 shorter events, 0.4 us)
Async XLA Ops:
  0.6 1.2 copy-start.1
  1.9 1.2 copy-start.2
  3.2 6.1 %collective-permute-start.20 = (f32[4,2,16,256]{3,2,1,0:T(8,128)S(1)}, f32[4,2,16,256]{3,2,1,0:T(8,128)S(1)}, u32[]{:S(2)}, u32[]{:S(2)}) collective-permute-start(f32[4,2,16,256]{3,2,1,0:T(8,128)S(1)} %get-tuple-element.82), channel_id=1, source_target_pairs={{0,1},{1,0},{2,3},{3,2},{4,5},{5,4},{6,7},{7,6},{8,9},{9,8},{10,11... | collective-permute-start | bytes 393224 | tf_op jit(solution)/shard_map/ppermute | solution.py:274
  3.3 9.3 %collective-permute-start.21 = (f32[4,2,16,256]{3,2,1,0:T(8,128)S(1)}, f32[4,2,16,256]{3,2,1,0:T(8,128)S(1)}, u32[]{:S(2)}, u32[]{:S(2)}) collective-permute-start(f32[4,2,16,256]{3,2,1,0:T(8,128)S(1)} %get-tuple-element.83), channel_id=1, source_target_pairs={{0,2},{1,3},{2,4},{3,5},{4,6},{5,7},{6,0},{7,1},{8,10},{9,11},{10,... | collective-permute-start | bytes 393224 | tf_op jit(solution)/shard_map/ppermute | solution.py:274
  4.9 9.5 %collective-permute-start.22 = (f32[4,2,16,256]{3,2,1,0:T(8,128)S(1)}, f32[4,2,16,256]{3,2,1,0:T(8,128)S(1)}, u32[]{:S(2)}, u32[]{:S(2)}) collective-permute-start(f32[4,2,16,256]{3,2,1,0:T(8,128)S(1)} %get-tuple-element.84), channel_id=1, source_target_pairs={{0,3},{1,2},{2,5},{3,4},{4,7},{5,6},{6,1},{7,0},{8,11},{9,10},{10,... | collective-permute-start | bytes 393224 | tf_op jit(solution)/shard_map/ppermute | solution.py:274
  6.1 11.5 %collective-permute-start.23 = (f32[4,2,16,256]{3,2,1,0:T(8,128)S(1)}, f32[4,2,16,256]{3,2,1,0:T(8,128)S(1)}, u32[]{:S(2)}, u32[]{:S(2)}) collective-permute-start(f32[4,2,16,256]{3,2,1,0:T(8,128)S(1)} %get-tuple-element.85), channel_id=1, source_target_pairs={{0,4},{1,5},{2,6},{3,7},{4,0},{5,1},{6,2},{7,3},{8,12},{9,13},{10,... | collective-permute-start | bytes 393224 | tf_op jit(solution)/shard_map/ppermute | solution.py:274
  7.8 16.9 %collective-permute-start.24 = (f32[4,2,16,256]{3,2,1,0:T(8,128)S(1)}, f32[4,2,16,256]{3,2,1,0:T(8,128)S(1)}, u32[]{:S(2)}, u32[]{:S(2)}) collective-permute-start(f32[4,2,16,256]{3,2,1,0:T(8,128)S(1)} %get-tuple-element.86), channel_id=1, source_target_pairs={{0,5},{1,4},{2,7},{3,6},{4,1},{5,0},{6,3},{7,2},{8,13},{9,12},{10,... | collective-permute-start | bytes 393224 | tf_op jit(solution)/shard_map/ppermute | solution.py:274
  9.4 20.7 %collective-permute-start = (f32[8,2,16,256]{3,2,1,0:T(8,128)S(1)}, f32[8,2,16,256]{3,2,1,0:T(8,128)S(1)}, u32[]{:S(2)}, u32[]{:S(2)}) collective-permute-start(f32[8,2,16,256]{3,2,1,0:T(8,128)S(1)} %get-tuple-element.57), channel_id=1, source_target_pairs={{0,8},{1,9},{2,10},{3,11},{4,12},{5,13},{6,14},{7,15},{8,16},{9,17... | collective-permute-start | bytes 786440 | tf_op jit(solution)/shard_map/ppermute | solution.py:262
  12.6 13.0 %collective-permute-start.25 = (f32[4,2,16,256]{3,2,1,0:T(8,128)S(1)}, f32[4,2,16,256]{3,2,1,0:T(8,128)S(1)}, u32[]{:S(2)}, u32[]{:S(2)}) collective-permute-start(f32[4,2,16,256]{3,2,1,0:T(8,128)S(1)} %get-tuple-element.87), channel_id=1, source_target_pairs={{0,6},{1,7},{2,0},{3,1},{4,2},{5,3},{6,4},{7,5},{8,14},{9,15},{10,... | collective-permute-start | bytes 393224 | tf_op jit(solution)/shard_map/ppermute | solution.py:274
  14.4 11.2 %collective-permute-start.26 = (f32[4,2,16,256]{3,2,1,0:T(8,128)S(1)}, f32[4,2,16,256]{3,2,1,0:T(8,128)S(1)}, u32[]{:S(2)}, u32[]{:S(2)}) collective-permute-start(f32[4,2,16,256]{3,2,1,0:T(8,128)S(1)} %get-tuple-element.88), channel_id=1, source_target_pairs={{0,7},{1,6},{2,1},{3,0},{4,3},{5,2},{6,5},{7,4},{8,15},{9,14},{10,... | collective-permute-start | bytes 393224 | tf_op jit(solution)/shard_map/ppermute | solution.py:274
  17.6 23.5 %collective-permute-start.1 = (f32[8,2,16,256]{3,2,1,0:T(8,128)S(1)}, f32[8,2,16,256]{3,2,1,0:T(8,128)S(1)}, u32[]{:S(2)}, u32[]{:S(2)}) collective-permute-start(f32[8,2,16,256]{3,2,1,0:T(8,128)S(1)} %get-tuple-element.58), channel_id=1, source_target_pairs={{0,16},{1,17},{2,18},{3,19},{4,20},{5,21},{6,22},{7,23},{8,24},{9,... | collective-permute-start | bytes 786440 | tf_op jit(solution)/shard_map/ppermute | solution.py:262
  24.8 39.8 %collective-permute-start.2 = (f32[8,2,16,256]{3,2,1,0:T(8,128)S(1)}, f32[8,2,16,256]{3,2,1,0:T(8,128)S(1)}, u32[]{:S(2)}, u32[]{:S(2)}) collective-permute-start(f32[8,2,16,256]{3,2,1,0:T(8,128)S(1)} %get-tuple-element.59), channel_id=1, source_target_pairs={{0,24},{1,25},{2,26},{3,27},{4,28},{5,29},{6,30},{7,31},{8,0},{9,1... | collective-permute-start | bytes 786440 | tf_op jit(solution)/shard_map/ppermute | solution.py:262
  25.6 48.1 %copy-start.6 = (bf16[8,256,256]{2,1,0:T(8,128)(2,1)S(1)}, bf16[8,256,256]{2,1,0:T(8,128)(2,1)}, u32[]{:S(2)}) copy-start(bf16[8,256,256]{2,1,0:T(8,128)(2,1)} %constant.6.clone.tab_ref) | copy-start | bytes 3145732
  25.7 39.2 %collective-permute-start.27 = (f32[8,2,16,256]{3,2,1,0:T(8,128)S(1)}, f32[8,2,16,256]{3,2,1,0:T(8,128)S(1)}, u32[]{:S(2)}, u32[]{:S(2)}) collective-permute-start(f32[8,2,16,256]{3,2,1,0:T(8,128)S(1)} %get-tuple-element.90), channel_id=1, source_target_pairs={{0,8},{1,9},{2,10},{3,11},{4,12},{5,13},{6,14},{7,15},{8,16},{9,17... | collective-permute-start | bytes 786440 | tf_op jit(solution)/shard_map/ppermute | solution.py:262
  27.9 37.5 %collective-permute-start.28 = (f32[8,2,16,256]{3,2,1,0:T(8,128)S(1)}, f32[8,2,16,256]{3,2,1,0:T(8,128)S(1)}, u32[]{:S(2)}, u32[]{:S(2)}) collective-permute-start(f32[8,2,16,256]{3,2,1,0:T(8,128)S(1)} %get-tuple-element.91), channel_id=1, source_target_pairs={{0,16},{1,17},{2,18},{3,19},{4,20},{5,21},{6,22},{7,23},{8,24},{9,... | collective-permute-start | bytes 786440 | tf_op jit(solution)/shard_map/ppermute | solution.py:262
  30.1 40.0 %collective-permute-start.29 = (f32[8,2,16,256]{3,2,1,0:T(8,128)S(1)}, f32[8,2,16,256]{3,2,1,0:T(8,128)S(1)}, u32[]{:S(2)}, u32[]{:S(2)}) collective-permute-start(f32[8,2,16,256]{3,2,1,0:T(8,128)S(1)} %get-tuple-element.92), channel_id=1, source_target_pairs={{0,24},{1,25},{2,26},{3,27},{4,28},{5,29},{6,30},{7,31},{8,0},{9,1... | collective-permute-start | bytes 786440 | tf_op jit(solution)/shard_map/ppermute | solution.py:262
  64.6 9.2 %copy-start.7 = (f32[256,2]{1,0:T(8,128)S(1)}, f32[256,2]{1,0:T(8,128)}, u32[]{:S(2)}) copy-start(f32[256,2]{1,0:T(8,128)} %constant.7.clone.sq_ref) | copy-start | bytes 6148
  64.7 5.8 %collective-permute-start.3 = (f32[4,2,16,256]{3,2,1,0:T(8,128)S(1)}, f32[4,2,16,256]{3,2,1,0:T(8,128)S(1)}, u32[]{:S(2)}, u32[]{:S(2)}) collective-permute-start(f32[4,2,16,256]{3,2,1,0:T(8,128)S(1)} %get-tuple-element.61), channel_id=1, source_target_pairs={{0,1},{1,0},{2,3},{3,2},{4,5},{5,4},{6,7},{7,6},{8,9},{9,8},{10,11... | collective-permute-start | bytes 393224 | tf_op jit(solution)/shard_map/ppermute | solution.py:274
  64.8 7.7 %collective-permute-start.4 = (f32[4,2,16,256]{3,2,1,0:T(8,128)S(1)}, f32[4,2,16,256]{3,2,1,0:T(8,128)S(1)}, u32[]{:S(2)}, u32[]{:S(2)}) collective-permute-start(f32[4,2,16,256]{3,2,1,0:T(8,128)S(1)} %get-tuple-element.62), channel_id=1, source_target_pairs={{0,2},{1,3},{2,4},{3,5},{4,6},{5,7},{6,0},{7,1},{8,10},{9,11},{10,... | collective-permute-start | bytes 393224 | tf_op jit(solution)/shard_map/ppermute | solution.py:274
  64.9 14.9 %collective-permute-start.5 = (f32[4,2,16,256]{3,2,1,0:T(8,128)S(1)}, f32[4,2,16,256]{3,2,1,0:T(8,128)S(1)}, u32[]{:S(2)}, u32[]{:S(2)}) collective-permute-start(f32[4,2,16,256]{3,2,1,0:T(8,128)S(1)} %get-tuple-element.63), channel_id=1, source_target_pairs={{0,3},{1,2},{2,5},{3,4},{4,7},{5,6},{6,1},{7,0},{8,11},{9,10},{10,... | collective-permute-start | bytes 393224 | tf_op jit(solution)/shard_map/ppermute | solution.py:274
  65.3 14.8 %collective-permute-start.6 = (f32[4,2,16,256]{3,2,1,0:T(8,128)S(1)}, f32[4,2,16,256]{3,2,1,0:T(8,128)S(1)}, u32[]{:S(2)}, u32[]{:S(2)}) collective-permute-start(f32[4,2,16,256]{3,2,1,0:T(8,128)S(1)} %get-tuple-element.64), channel_id=1, source_target_pairs={{0,4},{1,5},{2,6},{3,7},{4,0},{5,1},{6,2},{7,3},{8,12},{9,13},{10,... | collective-permute-start | bytes 393224 | tf_op jit(solution)/shard_map/ppermute | solution.py:274
  70.1 10.0 %collective-permute-start.7 = (f32[4,2,16,256]{3,2,1,0:T(8,128)S(1)}, f32[4,2,16,256]{3,2,1,0:T(8,128)S(1)}, u32[]{:S(2)}, u32[]{:S(2)}) collective-permute-start(f32[4,2,16,256]{3,2,1,0:T(8,128)S(1)} %get-tuple-element.65), channel_id=1, source_target_pairs={{0,5},{1,4},{2,7},{3,6},{4,1},{5,0},{6,3},{7,2},{8,13},{9,12},{10,... | collective-permute-start | bytes 393224 | tf_op jit(solution)/shard_map/ppermute | solution.py:274
  70.5 3.2 %copy-start.8 = (f32[2,256]{1,0:T(2,128)S(1)}, f32[2,256]{1,0:T(2,128)}, u32[]{:S(2)}) copy-start(f32[2,256]{1,0:T(2,128)} %constant.8.clone.sqt_ref) | copy-start | bytes 6148
  70.5 9.7 %collective-permute-start.8 = (f32[4,2,16,256]{3,2,1,0:T(8,128)S(1)}, f32[4,2,16,256]{3,2,1,0:T(8,128)S(1)}, u32[]{:S(2)}, u32[]{:S(2)}) collective-permute-start(f32[4,2,16,256]{3,2,1,0:T(8,128)S(1)} %get-tuple-element.66), channel_id=1, source_target_pairs={{0,6},{1,7},{2,0},{3,1},{4,2},{5,3},{6,4},{7,5},{8,14},{9,15},{10,... | collective-permute-start | bytes 393224 | tf_op jit(solution)/shard_map/ppermute | solution.py:274
  72.4 1.3 copy-start.3
  72.4 1.3 copy-start.4
  72.4 1.3 copy-start.5
  72.4 11.9 %collective-permute-start.9 = (f32[4,2,16,256]{3,2,1,0:T(8,128)S(1)}, f32[4,2,16,256]{3,2,1,0:T(8,128)S(1)}, u32[]{:S(2)}, u32[]{:S(2)}) collective-permute-start(f32[4,2,16,256]{3,2,1,0:T(8,128)S(1)} %get-tuple-element.67), channel_id=1, source_target_pairs={{0,7},{1,6},{2,1},{3,0},{4,3},{5,2},{6,5},{7,4},{8,15},{9,14},{10,... | collective-permute-start | bytes 393224 | tf_op jit(solution)/shard_map/ppermute | solution.py:274
  79.7 8.6 %collective-permute-start.30 = (f32[4,2,16,256]{3,2,1,0:T(8,128)S(1)}, f32[4,2,16,256]{3,2,1,0:T(8,128)S(1)}, u32[]{:S(2)}, u32[]{:S(2)}) collective-permute-start(f32[4,2,16,256]{3,2,1,0:T(8,128)S(1)} %get-tuple-element.94), channel_id=1, source_target_pairs={{0,1},{1,0},{2,3},{3,2},{4,5},{5,4},{6,7},{7,6},{8,9},{9,8},{10,11... | collective-permute-start | bytes 393224 | tf_op jit(solution)/shard_map/ppermute | solution.py:274
  80.1 8.8 %collective-permute-start.31 = (f32[4,2,16,256]{3,2,1,0:T(8,128)S(1)}, f32[4,2,16,256]{3,2,1,0:T(8,128)S(1)}, u32[]{:S(2)}, u32[]{:S(2)}) collective-permute-start(f32[4,2,16,256]{3,2,1,0:T(8,128)S(1)} %get-tuple-element.95), channel_id=1, source_target_pairs={{0,2},{1,3},{2,4},{3,5},{4,6},{5,7},{6,0},{7,1},{8,10},{9,11},{10,... | collective-permute-start | bytes 393224 | tf_op jit(solution)/shard_map/ppermute | solution.py:274
  80.1 14.3 %collective-permute-start.32 = (f32[4,2,16,256]{3,2,1,0:T(8,128)S(1)}, f32[4,2,16,256]{3,2,1,0:T(8,128)S(1)}, u32[]{:S(2)}, u32[]{:S(2)}) collective-permute-start(f32[4,2,16,256]{3,2,1,0:T(8,128)S(1)} %get-tuple-element.96), channel_id=1, source_target_pairs={{0,3},{1,2},{2,5},{3,4},{4,7},{5,6},{6,1},{7,0},{8,11},{9,10},{10,... | collective-permute-start | bytes 393224 | tf_op jit(solution)/shard_map/ppermute | solution.py:274
  80.2 14.2 %collective-permute-start.33 = (f32[4,2,16,256]{3,2,1,0:T(8,128)S(1)}, f32[4,2,16,256]{3,2,1,0:T(8,128)S(1)}, u32[]{:S(2)}, u32[]{:S(2)}) collective-permute-start(f32[4,2,16,256]{3,2,1,0:T(8,128)S(1)} %get-tuple-element.97), channel_id=1, source_target_pairs={{0,4},{1,5},{2,6},{3,7},{4,0},{5,1},{6,2},{7,3},{8,12},{9,13},{10,... | collective-permute-start | bytes 393224 | tf_op jit(solution)/shard_map/ppermute | solution.py:274
  84.3 12.9 %collective-permute-start.34 = (f32[4,2,16,256]{3,2,1,0:T(8,128)S(1)}, f32[4,2,16,256]{3,2,1,0:T(8,128)S(1)}, u32[]{:S(2)}, u32[]{:S(2)}) collective-permute-start(f32[4,2,16,256]{3,2,1,0:T(8,128)S(1)} %get-tuple-element.98), channel_id=1, source_target_pairs={{0,5},{1,4},{2,7},{3,6},{4,1},{5,0},{6,3},{7,2},{8,13},{9,12},{10,... | collective-permute-start | bytes 393224 | tf_op jit(solution)/shard_map/ppermute | solution.py:274
  88.3 17.0 %collective-permute-start.10 = (f32[8,2,16,256]{3,2,1,0:T(8,128)S(1)}, f32[8,2,16,256]{3,2,1,0:T(8,128)S(1)}, u32[]{:S(2)}, u32[]{:S(2)}) collective-permute-start(f32[8,2,16,256]{3,2,1,0:T(8,128)S(1)} %get-tuple-element.69), channel_id=1, source_target_pairs={{0,8},{1,9},{2,10},{3,11},{4,12},{5,13},{6,14},{7,15},{8,16},{9,17... | collective-permute-start | bytes 786440 | tf_op jit(solution)/shard_map/ppermute | solution.py:262
  89.0 9.6 %collective-permute-start.35 = (f32[4,2,16,256]{3,2,1,0:T(8,128)S(1)}, f32[4,2,16,256]{3,2,1,0:T(8,128)S(1)}, u32[]{:S(2)}, u32[]{:S(2)}) collective-permute-start(f32[4,2,16,256]{3,2,1,0:T(8,128)S(1)} %get-tuple-element.99), channel_id=1, source_target_pairs={{0,6},{1,7},{2,0},{3,1},{4,2},{5,3},{6,4},{7,5},{8,14},{9,15},{10,... | collective-permute-start | bytes 393224 | tf_op jit(solution)/shard_map/ppermute | solution.py:274
  94.5 4.7 %collective-permute-start.36 = (f32[4,2,16,256]{3,2,1,0:T(8,128)S(1)}, f32[4,2,16,256]{3,2,1,0:T(8,128)S(1)}, u32[]{:S(2)}, u32[]{:S(2)}) collective-permute-start(f32[4,2,16,256]{3,2,1,0:T(8,128)S(1)} %get-tuple-element.100), channel_id=1, source_target_pairs={{0,7},{1,6},{2,1},{3,0},{4,3},{5,2},{6,5},{7,4},{8,15},{9,14},{10,... | collective-permute-start | bytes 393224 | tf_op jit(solution)/shard_map/ppermute | solution.py:274
  94.5 24.5 %collective-permute-start.11 = (f32[8,2,16,256]{3,2,1,0:T(8,128)S(1)}, f32[8,2,16,256]{3,2,1,0:T(8,128)S(1)}, u32[]{:S(2)}, u32[]{:S(2)}) collective-permute-start(f32[8,2,16,256]{3,2,1,0:T(8,128)S(1)} %get-tuple-element.70), channel_id=1, source_target_pairs={{0,16},{1,17},{2,18},{3,19},{4,20},{5,21},{6,22},{7,23},{8,24},{9,... | collective-permute-start | bytes 786440 | tf_op jit(solution)/shard_map/ppermute | solution.py:262
  97.2 41.3 %collective-permute-start.12 = (f32[8,2,16,256]{3,2,1,0:T(8,128)S(1)}, f32[8,2,16,256]{3,2,1,0:T(8,128)S(1)}, u32[]{:S(2)}, u32[]{:S(2)}) collective-permute-start(f32[8,2,16,256]{3,2,1,0:T(8,128)S(1)} %get-tuple-element.71), channel_id=1, source_target_pairs={{0,24},{1,25},{2,26},{3,27},{4,28},{5,29},{6,30},{7,31},{8,0},{9,1... | collective-permute-start | bytes 786440 | tf_op jit(solution)/shard_map/ppermute | solution.py:262
  99.1 48.9 %copy-start = (f32[32,16,512]{2,1,0:T(8,128)S(1)}, f32[32,16,512]{2,1,0:T(8,128)}, u32[]{:S(2)}) copy-start(f32[32,16,512]{2,1,0:T(8,128)} %w_ref.1) | copy-start | bytes 3145732
  99.2 41.1 %collective-permute-start.37 = (f32[8,2,16,256]{3,2,1,0:T(8,128)S(1)}, f32[8,2,16,256]{3,2,1,0:T(8,128)S(1)}, u32[]{:S(2)}, u32[]{:S(2)}) collective-permute-start(f32[8,2,16,256]{3,2,1,0:T(8,128)S(1)} %get-tuple-element.102), channel_id=1, source_target_pairs={{0,8},{1,9},{2,10},{3,11},{4,12},{5,13},{6,14},{7,15},{8,16},{9,17... | collective-permute-start | bytes 786440 | tf_op jit(solution)/shard_map/ppermute | solution.py:262
  100.6 39.7 %collective-permute-start.38 = (f32[8,2,16,256]{3,2,1,0:T(8,128)S(1)}, f32[8,2,16,256]{3,2,1,0:T(8,128)S(1)}, u32[]{:S(2)}, u32[]{:S(2)}) collective-permute-start(f32[8,2,16,256]{3,2,1,0:T(8,128)S(1)} %get-tuple-element.103), channel_id=1, source_target_pairs={{0,16},{1,17},{2,18},{3,19},{4,20},{5,21},{6,22},{7,23},{8,24},{9,... | collective-permute-start | bytes 786440 | tf_op jit(solution)/shard_map/ppermute | solution.py:262
  105.3 38.8 %collective-permute-start.39 = (f32[8,2,16,256]{3,2,1,0:T(8,128)S(1)}, f32[8,2,16,256]{3,2,1,0:T(8,128)S(1)}, u32[]{:S(2)}, u32[]{:S(2)}) collective-permute-start(f32[8,2,16,256]{3,2,1,0:T(8,128)S(1)} %get-tuple-element.104), channel_id=1, source_target_pairs={{0,24},{1,25},{2,26},{3,27},{4,28},{5,29},{6,30},{7,31},{8,0},{9,1... | collective-permute-start | bytes 786440 | tf_op jit(solution)/shard_map/ppermute | solution.py:262
  138.6 5.6 %collective-permute-start.13 = (f32[4,2,16,256]{3,2,1,0:T(8,128)S(1)}, f32[4,2,16,256]{3,2,1,0:T(8,128)S(1)}, u32[]{:S(2)}, u32[]{:S(2)}) collective-permute-start(f32[4,2,16,256]{3,2,1,0:T(8,128)S(1)} %get-tuple-element.73), channel_id=1, source_target_pairs={{0,1},{1,0},{2,3},{3,2},{4,5},{5,4},{6,7},{7,6},{8,9},{9,8},{10,11... | collective-permute-start | bytes 393224 | tf_op jit(solution)/shard_map/ppermute | solution.py:274
  138.8 9.1 %collective-permute-start.14 = (f32[4,2,16,256]{3,2,1,0:T(8,128)S(1)}, f32[4,2,16,256]{3,2,1,0:T(8,128)S(1)}, u32[]{:S(2)}, u32[]{:S(2)}) collective-permute-start(f32[4,2,16,256]{3,2,1,0:T(8,128)S(1)} %get-tuple-element.74), channel_id=1, source_target_pairs={{0,2},{1,3},{2,4},{3,5},{4,6},{5,7},{6,0},{7,1},{8,10},{9,11},{10,... | collective-permute-start | bytes 393224 | tf_op jit(solution)/shard_map/ppermute | solution.py:274
  140.3 13.4 %collective-permute-start.15 = (f32[4,2,16,256]{3,2,1,0:T(8,128)S(1)}, f32[4,2,16,256]{3,2,1,0:T(8,128)S(1)}, u32[]{:S(2)}, u32[]{:S(2)}) collective-permute-start(f32[4,2,16,256]{3,2,1,0:T(8,128)S(1)} %get-tuple-element.75), channel_id=1, source_target_pairs={{0,3},{1,2},{2,5},{3,4},{4,7},{5,6},{6,1},{7,0},{8,11},{9,10},{10,... | collective-permute-start | bytes 393224 | tf_op jit(solution)/shard_map/ppermute | solution.py:274
  140.3 16.2 %collective-permute-start.16 = (f32[4,2,16,256]{3,2,1,0:T(8,128)S(1)}, f32[4,2,16,256]{3,2,1,0:T(8,128)S(1)}, u32[]{:S(2)}, u32[]{:S(2)}) collective-permute-start(f32[4,2,16,256]{3,2,1,0:T(8,128)S(1)} %get-tuple-element.76), channel_id=1, source_target_pairs={{0,4},{1,5},{2,6},{3,7},{4,0},{5,1},{6,2},{7,3},{8,12},{9,13},{10,... | collective-permute-start | bytes 393224 | tf_op jit(solution)/shard_map/ppermute | solution.py:274
  144.1 17.6 %collective-permute-start.17 = (f32[4,2,16,256]{3,2,1,0:T(8,128)S(1)}, f32[4,2,16,256]{3,2,1,0:T(8,128)S(1)}, u32[]{:S(2)}, u32[]{:S(2)}) collective-permute-start(f32[4,2,16,256]{3,2,1,0:T(8,128)S(1)} %get-tuple-element.77), channel_id=1, source_target_pairs={{0,5},{1,4},{2,7},{3,6},{4,1},{5,0},{6,3},{7,2},{8,13},{9,12},{10,... | collective-permute-start | bytes 393224 | tf_op jit(solution)/shard_map/ppermute | solution.py:274
  144.2 19.6 %collective-permute-start.18 = (f32[4,2,16,256]{3,2,1,0:T(8,128)S(1)}, f32[4,2,16,256]{3,2,1,0:T(8,128)S(1)}, u32[]{:S(2)}, u32[]{:S(2)}) collective-permute-start(f32[4,2,16,256]{3,2,1,0:T(8,128)S(1)} %get-tuple-element.78), channel_id=1, source_target_pairs={{0,6},{1,7},{2,0},{3,1},{4,2},{5,3},{6,4},{7,5},{8,14},{9,15},{10,... | collective-permute-start | bytes 393224 | tf_op jit(solution)/shard_map/ppermute | solution.py:274
  147.8 19.8 %collective-permute-start.19 = (f32[4,2,16,256]{3,2,1,0:T(8,128)S(1)}, f32[4,2,16,256]{3,2,1,0:T(8,128)S(1)}, u32[]{:S(2)}, u32[]{:S(2)}) collective-permute-start(f32[4,2,16,256]{3,2,1,0:T(8,128)S(1)} %get-tuple-element.79), channel_id=1, source_target_pairs={{0,7},{1,6},{2,1},{3,0},{4,3},{5,2},{6,5},{7,4},{8,15},{9,14},{10,... | collective-permute-start | bytes 393224 | tf_op jit(solution)/shard_map/ppermute | solution.py:274
  153.7 18.1 %collective-permute-start.45 = (f32[16,512]{1,0:T(8,128)S(1)}, f32[16,512]{1,0:T(8,128)S(1)}, u32[]{:S(2)}, u32[]{:S(2)}) collective-permute-start(f32[16,512]{1,0:T(8,128)S(1)} %get-tuple-element.110), channel_id=1, source_target_pairs={{32,0},{64,32},{96,64},{128,96},{160,128},{192,160},{224,192},{33,... | collective-permute-start | bytes 98312 | tf_op jit(solution)/shard_map/ppermute | solution.py:278
  156.5 17.3 %collective-permute-start.44 = (f32[16,512]{1,0:T(8,128)S(1)}, f32[16,512]{1,0:T(8,128)S(1)}, u32[]{:S(2)}, u32[]{:S(2)}) collective-permute-start(f32[16,512]{1,0:T(8,128)S(1)} %get-tuple-element.111), channel_id=1, source_target_pairs={{0,32},{32,64},{64,96},{96,128},{128,160},{160,192},{192,224},{1,3... | collective-permute-start | bytes 98312 | tf_op jit(solution)/shard_map/ppermute | solution.py:278
  161.8 12.0 %collective-permute-start.42 = (f32[2,16,256]{2,1,0:T(8,128)S(1)}, f32[2,16,256]{2,1,0:T(8,128)S(1)}, u32[]{:S(2)}, u32[]{:S(2)}) collective-permute-start(f32[2,16,256]{2,1,0:T(8,128)S(1)} %get-tuple-element.108), channel_id=1, source_target_pairs={{0,32},{32,64},{64,96},{96,128},{128,160},{160,192},{192,224},{1,3... | collective-permute-start | bytes 98312 | tf_op jit(solution)/shard_map/ppermute | solution.py:278
  163.7 10.1 %collective-permute-start.43 = (f32[2,16,256]{2,1,0:T(8,128)S(1)}, f32[2,16,256]{2,1,0:T(8,128)S(1)}, u32[]{:S(2)}, u32[]{:S(2)}) collective-permute-start(f32[2,16,256]{2,1,0:T(8,128)S(1)} %get-tuple-element.109), channel_id=1, source_target_pairs={{32,0},{64,32},{96,64},{128,96},{160,128},{192,160},{224,192},{33,... | collective-permute-start | bytes 98312 | tf_op jit(solution)/shard_map/ppermute | solution.py:278
  167.8 6.0 %collective-permute-start.40 = (f32[2,16,256]{2,1,0:T(8,128)S(1)}, f32[2,16,256]{2,1,0:T(8,128)S(1)}, u32[]{:S(2)}, u32[]{:S(2)}) collective-permute-start(f32[2,16,256]{2,1,0:T(8,128)S(1)} %get-tuple-element.106), channel_id=1, source_target_pairs={{0,32},{32,64},{64,96},{96,128},{128,160},{160,192},{192,224},{1,3... | collective-permute-start | bytes 98312 | tf_op jit(solution)/shard_map/ppermute | solution.py:278
  171.8 7.9 %collective-permute-start.41 = (f32[2,16,256]{2,1,0:T(8,128)S(1)}, f32[2,16,256]{2,1,0:T(8,128)S(1)}, u32[]{:S(2)}, u32[]{:S(2)}) collective-permute-start(f32[2,16,256]{2,1,0:T(8,128)S(1)} %get-tuple-element.107), channel_id=1, source_target_pairs={{32,0},{64,32},{96,64},{128,96},{160,128},{192,160},{224,192},{33,... | collective-permute-start | bytes 98312 | tf_op jit(solution)/shard_map/ppermute | solution.py:278

commit v3 on v2

--- a/solution.py
+++ b/solution.py
@@ -106,6 +106,16 @@
     gathered(pieces, out_ref)
     first_ref[...] = out_ref[0]
     last_ref[...] = out_ref[out_ref.shape[0] - 1]
+
+
+def unpack_with_speed_kernel(w_first_ref, w_last_ref, *refs):
+    pieces, (out_ref, first_ref, last_ref) = refs[:-3], refs[-3:]
+    gathered(pieces, out_ref)
+    half = out_ref.shape[-1]
+    for edge_ref, w_ref, level in ((first_ref, w_first_ref, 0), (last_ref, w_last_ref, out_ref.shape[0] - 1)):
+        edge_ref[:2] = out_ref[level]
+        edge_ref[2] = w_ref[0, :, :half]
+        edge_ref[3] = w_ref[0, :, half:]
 
 
 def transformed(parity, rates, x_ref, tab_ref, sq_ref, sqt_ref):
@@ -178,42 +188,68 @@
                 outs[near][step] = block
 
 
-def flux_kernel(
-    even_ref, odd_ref, w_ref, elow_ref, ehigh_ref, olow_ref, ohigh_ref, wlow_ref, whigh_ref, t_out, s_out
-):
+def unfolded(even, odd):
+    return tuple(jnp.concatenate([even[f] + odd[f], even[f] - odd[f]], axis=-1) for f in (0, 1))
+
+
+def face(lower, upper):
+    lt, ls, lw = lower
+    ut, us, uw = upper
+    flow = 0.5 * (lw + uw) + buoyancy * 0.5 * ((lt + ut) - (ls + us))
+    up = jnp.maximum(flow, 0.0)
+    down = jnp.minimum(flow, 0.0)
+    return up * lt + down * ut, up * ls + down * us
+
+
+def inner_flux_kernel(even_ref, odd_ref, w_ref, t_out, s_out, t_first, s_first, t_last, s_last):
     levels = w_ref.shape[0]
-    block = lax.axis_index("lev")
-    last = lax.axis_size("lev") - 1
-
-    def unfolded(even, odd):
-        return tuple(
-            jnp.concatenate([even[f] + odd[f], even[f] - odd[f]], axis=-1) for f in (0, 1)
-        )
 
     def at_level(level):
         return unfolded(even_ref[level], odd_ref[level]) + (w_ref[level],)
 
-    def face(lower, upper):
-        lt, ls, lw = lower
-        ut, us, uw = upper
-        flow = 0.5 * (lw + uw) + buoyancy * 0.5 * ((lt + ut) - (ls + us))
-        up = jnp.maximum(flow, 0.0)
-        down = jnp.minimum(flow, 0.0)
-        return up * lt + down * ut, up * ls + down * us
-
     at = at_level(0)
-    below = face(unfolded(elow_ref[...], olow_ref[...]) + (wlow_ref[...],), at)
-    below = tuple(jnp.where(block > 0, b, 0.0) for b in below)
-    for level in range(levels):
-        if level + 1 < levels:
-            nxt = at_level(level + 1)
-            above = face(at, nxt)
-        else:
-            nxt = unfolded(ehigh_ref[...], ohigh_ref[...]) + (whigh_ref[...],)
-            above = tuple(jnp.where(block < last, a, 0.0) for a in face(at, nxt))
+    t_first[0], s_first[0] = at[0], at[1]
+    below = (jnp.zeros_like(at[0]),) * 2
+
+    def body(level, carried):
+        at, below = carried[:3], carried[3:]
+        nxt = at_level(level + 1)
+        above = face(at, nxt)
         t_out[level] = at[0] - advective_number * (above[0] - below[0])
         s_out[level] = at[1] - advective_number * (above[1] - below[1])
-        at, below = nxt, above
+        return nxt + above
+
+    carried = at + below
+    carried = lax.fori_loop(0, levels - 1, body, carried)
+    at, below = carried[:3], carried[3:]
+    t_last[0], s_last[0] = at[0], at[1]
+    t_out[levels - 1] = at[0] + advective_number * below[0]
+    s_out[levels - 1] = at[1] + advective_number * below[1]
+
+
+def outer_flux_kernel(
+    t_ref, s_ref, tf_ref, sf_ref, tl_ref, sl_ref, wf_ref, wl_ref, elow, ehigh, olow, ohigh, t_out, s_out
+):
+    block = lax.axis_index("lev")
+    edge = pl.program_id(0)
+
+    def speed(ref):
+        return jnp.concatenate([ref[2], ref[3]], axis=-1)
+
+    @pl.when(edge == 0)
+    def _():
+        other = unfolded(elow[...], olow[...]) + (speed(elow),)
+        flux = face(other, (tf_ref[0], sf_ref[0], wf_ref[0]))
+        t_out[0] = t_ref[0] + advective_number * jnp.where(block > 0, flux[0], 0.0)
+        s_out[0] = s_ref[0] + advective_number * jnp.where(block > 0, flux[1], 0.0)
+
+    @pl.when(edge == 1)
+    def _():
+        other = unfolded(ehigh[...], ohigh[...]) + (speed(ehigh),)
+        flux = face((tl_ref[0], sl_ref[0], wl_ref[0]), other)
+        is_open = block < lax.axis_size("lev") - 1
+        t_out[0] = t_ref[0] - advective_number * jnp.where(is_open, flux[0], 0.0)
+        s_out[0] = s_ref[0] - advective_number * jnp.where(is_open, flux[1], 0.0)
 
 
 def constants(length):
@@ -230,12 +266,13 @@
 smem = pl.BlockSpec(memory_space=pltpu.SMEM)
 
 
-def call(kernel, outs, *args, smem_args=0, scratch=(), flops=0):
+def call(kernel, outs, *args, smem_args=0, scratch=(), flops=0, specs=None, grid=()):
     moved = sum(math.prod(a.shape) * 4 for a in args) + sum(math.prod(o.shape) * 4 for o in outs)
     return pl.pallas_call(
         kernel,
         out_shape=tuple(outs),
-        in_specs=[smem] * smem_args + [vmem] * (len(args) - smem_args),
+        grid=grid,
+        in_specs=specs or [smem] * smem_args + [vmem] * (len(args) - smem_args),
         out_specs=(vmem,) * len(outs),
         scratch_shapes=scratch,
         compiler_params=pltpu.CompilerParams(vmem_limit_bytes=24 << 20),
@@ -299,19 +336,38 @@
     even, odd = folded[:4], folded[4:]
     even = along_z(even)
     odd = in_plane(odd)
-    w_halo = halo(updraft[0], updraft[-1])
     odd = along_z(repacked(odd))
     even = in_plane(repacked(even))
     even = along_z(solved(0, even))
     odd = in_plane(solved(1, odd))
     odd = along_z(repacked(odd))
     even = in_plane(repacked(even))
-    even, *even_ends = kernel(unpack_kernel, [whole, edge, edge], *even)
+    first_level = pl.BlockSpec((1, rows, length), lambda *_: (0, 0, 0))
+    last_level = pl.BlockSpec((1, rows, length), lambda *_: (levels - 1, 0, 0))
+    edge_with_speed = jax.ShapeDtypeStruct((4, rows, half), f32)
+    even, *even_ends = kernel(
+        unpack_with_speed_kernel, [whole, edge_with_speed, edge_with_speed], updraft, updraft, *even,
+        specs=[first_level, last_level] + [vmem] * 8, grid=(1,),
+    )
     even_halo = halo(*even_ends)
     odd, *odd_ends = kernel(unpack_kernel, [whole, edge, edge], *odd)
     odd_halo = halo(*odd_ends)
     field = jax.ShapeDtypeStruct(heat.shape, f32)
-    return kernel(flux_kernel, [field, field], even, odd, updraft, *even_halo, *odd_halo, *w_halo)
+    one = jax.ShapeDtypeStruct((1, rows, length), f32)
+    temp, salt, *ends = kernel(inner_flux_kernel, [field, field, one, one, one, one], even, odd, updraft)
+    both_ends = pl.BlockSpec((1, rows, length), lambda i: (i * (levels - 1), 0, 0))
+    return pl.pallas_call(
+        outer_flux_kernel,
+        grid=(2,),
+        out_shape=(field, field),
+        in_specs=[both_ends] * 2 + [vmem] * 4 + [
+            pl.BlockSpec((1, rows, length), lambda i: (0, 0, 0)),
+            pl.BlockSpec((1, rows, length), lambda i: (levels - 1, 0, 0)),
+        ] + [vmem] * 4,
+        out_specs=(both_ends, both_ends),
+        input_output_aliases={0: 0, 1: 1},
+        name="outer",
+    )(temp, salt, *ends, updraft, updraft, *even_halo, *odd_halo)
 
 
 def solution(mesh):

time: 182 us -> 162 us (0.89)
  the two profiles are of different devices: /device:TPU:24 before, /device:TPU:34 now
where the time goes in v3:
time: 162 us; the launch traced here: 161 us
  starting transfers between devices  80.1 us (49%)
  waiting for transfers between devices  62.4 us (39%)
  Pallas kernels  12.3 us (8%)
  local copies, waits for them, and re-layouts  5.53 us (3%)
    ppermute x28, waiting for transfers between devices, in_plane(): out.append(lax.ppermute(pieces[near], 'hor', pairs))  43.8 us
    ppermute x28, starting transfers between devices, in_plane(): out.append(lax.ppermute(pieces[near], 'hor', pairs))  32.2 us
    ppermute x12, starting transfers between devices, along_z(): out.append(lax.ppermute(pieces[step], 'hor', pairs))  30.1 us
    ppermute x12, waiting for transfers between devices, along_z(): out.append(lax.ppermute(pieces[step], 'hor', pairs))  18.7 us
    ppermute x2, starting transfers between devices, halo(): lax.ppermute(first, 'lev', downward)  10.8 us
    pallas_call x10, Pallas kernels, call(): pl.pallas_call(kernel, out_shape=tuple(outs), grid=grid, in_specs=specs o...  10.5 us
    ppermute x2, starting transfers between devices, halo(): lax.ppermute(last, 'lev', upward)  6.99 us
    unnamed x34, local copies, waits for them, and re-layouts  5.53 us
  transfers between devices with their start and end apart: 44, of which 17 were waited for; matrix products, arithmetic and copies ran while one was open for 0% of the time, Pallas kernels for 6%

profile of v3, /device:TPU:34, one launch (start us, length us, event | category | flops | bytes accessed | tf_op | source)
XLA Modules:
  0.0 161.4 jit_solution(15556158538833107517)
XLA Ops:
  0.6 1.2 copy-done.1
  1.9 1.2 copy-done.2
  3.1 0.1 shard_map.104
  3.2 3.3 %collective-permute-start = (f32[8,2,16,256]{3,2,1,0:T(8,128)S(1)}, f32[8,2,16,256]{3,2,1,0:T(8,128)S(1)}, u32[]{:S(2)}, u32[]{:S(2)}) collective-permute-start(f32[8,2,16,256]{3,2,1,0:T(8,128)S(1)} %get-tuple-element.63), channel_id=1, source_target_pairs={{0,8},{1,9},{2,10},{3,11},{4,12},{5,13},{6,14},{7,15},{8,16},{9,17... | collective-permute-start | bytes 786440 | tf_op jit(solution)/shard_map/ppermute | solution.py:299
  6.6 4.5 %collective-permute-start.1 = (f32[8,2,16,256]{3,2,1,0:T(8,128)S(1)}, f32[8,2,16,256]{3,2,1,0:T(8,128)S(1)}, u32[]{:S(2)}, u32[]{:S(2)}) collective-permute-start(f32[8,2,16,256]{3,2,1,0:T(8,128)S(1)} %get-tuple-element.64), channel_id=1, source_target_pairs={{0,16},{1,17},{2,18},{3,19},{4,20},{5,21},{6,22},{7,23},{8,24},{9,... | collective-permute-start | bytes 786440 | tf_op jit(solution)/shard_map/ppermute | solution.py:299
  11.1 2.7 %collective-permute-start.2 = (f32[8,2,16,256]{3,2,1,0:T(8,128)S(1)}, f32[8,2,16,256]{3,2,1,0:T(8,128)S(1)}, u32[]{:S(2)}, u32[]{:S(2)}) collective-permute-start(f32[8,2,16,256]{3,2,1,0:T(8,128)S(1)} %get-tuple-element.65), channel_id=1, source_target_pairs={{0,24},{1,25},{2,26},{3,27},{4,28},{5,29},{6,30},{7,31},{8,0},{9,1... | collective-permute-start | bytes 786440 | tf_op jit(solution)/shard_map/ppermute | solution.py:299
  13.7 1.5 collective-permute-start.21
  15.2 1.1 collective-permute-start.22
  16.3 3.8 %collective-permute-done.21.refs_2_ = f32[4,2,16,256]{3,2,1,0:T(8,128)S(1)} collective-permute-done((f32[4,2,16,256]{3,2,1,0:T(8,128)S(1)}, f32[4,2,16,256]{3,2,1,0:T(8,128)S(1)}, u32[]{:S(2)}, u32[]{:S(2)}) %collective-permute-start.21) | collective-permute-done | bytes 131104 | tf_op jit(solution)/shard_map/ppermute | solution.py:311
  20.1 2.1 %collective-permute-start.23 = (f32[4,2,16,256]{3,2,1,0:T(8,128)S(1)}, f32[4,2,16,256]{3,2,1,0:T(8,128)S(1)}, u32[]{:S(2)}, u32[]{:S(2)}) collective-permute-start(f32[4,2,16,256]{3,2,1,0:T(8,128)S(1)} %get-tuple-element.91), channel_id=1, source_target_pairs={{0,4},{1,5},{2,6},{3,7},{4,0},{5,1},{6,2},{7,3},{8,12},{9,13},{10,... | collective-permute-start | bytes 393224 | tf_op jit(solution)/shard_map/ppermute | solution.py:311
  22.2 5.7 %collective-permute-done.refs_1_ = f32[8,2,16,256]{3,2,1,0:T(8,128)S(1)} collective-permute-done((f32[8,2,16,256]{3,2,1,0:T(8,128)S(1)}, f32[8,2,16,256]{3,2,1,0:T(8,128)S(1)}, u32[]{:S(2)}, u32[]{:S(2)}) %collective-permute-start) | collective-permute-done | bytes 262176 | tf_op jit(solution)/shard_map/ppermute | solution.py:299
  27.9 0.7 collective-permute-start.24
  28.6 1.4 collective-permute-start.25
  30.1 2.0 %collective-permute-start.26 = (f32[4,2,16,256]{3,2,1,0:T(8,128)S(1)}, f32[4,2,16,256]{3,2,1,0:T(8,128)S(1)}, u32[]{:S(2)}, u32[]{:S(2)}) collective-permute-start(f32[4,2,16,256]{3,2,1,0:T(8,128)S(1)} %get-tuple-element.94), channel_id=1, source_target_pairs={{0,7},{1,6},{2,1},{3,0},{4,3},{5,2},{6,5},{7,4},{8,15},{9,14},{10,... | collective-permute-start | bytes 393224 | tf_op jit(solution)/shard_map/ppermute | solution.py:311
  32.2 1.0 collective-permute-start.4
  33.2 2.0 %collective-permute-done.24.refs_5_ = f32[4,2,16,256]{3,2,1,0:T(8,128)S(1)} collective-permute-done((f32[4,2,16,256]{3,2,1,0:T(8,128)S(1)}, f32[4,2,16,256]{3,2,1,0:T(8,128)S(1)}, u32[]{:S(2)}, u32[]{:S(2)}) %collective-permute-start.24) | collective-permute-done | bytes 131104 | tf_op jit(solution)/shard_map/ppermute | solution.py:311
  35.2 1.9 %collective-permute-done.25.refs_6_ = f32[4,2,16,256]{3,2,1,0:T(8,128)S(1)} collective-permute-done((f32[4,2,16,256]{3,2,1,0:T(8,128)S(1)}, f32[4,2,16,256]{3,2,1,0:T(8,128)S(1)}, u32[]{:S(2)}, u32[]{:S(2)}) %collective-permute-start.25) | collective-permute-done | bytes 131104 | tf_op jit(solution)/shard_map/ppermute | solution.py:311
  37.1 2.1 %collective-permute-start.6 = (f32[4,2,16,256]{3,2,1,0:T(8,128)S(1)}, f32[4,2,16,256]{3,2,1,0:T(8,128)S(1)}, u32[]{:S(2)}, u32[]{:S(2)}) collective-permute-start(f32[4,2,16,256]{3,2,1,0:T(8,128)S(1)} %get-tuple-element.70), channel_id=1, source_target_pairs={{0,4},{1,5},{2,6},{3,7},{4,0},{5,1},{6,2},{7,3},{8,12},{9,13},{10,... | collective-permute-start | bytes 393224 | tf_op jit(solution)/shard_map/ppermute | solution.py:311
  39.2 0.8 collective-permute-done.26.refs_7_
  40.0 1.8 %collective-permute-start.7 = (f32[4,2,16,256]{3,2,1,0:T(8,128)S(1)}, f32[4,2,16,256]{3,2,1,0:T(8,128)S(1)}, u32[]{:S(2)}, u32[]{:S(2)}) collective-permute-start(f32[4,2,16,256]{3,2,1,0:T(8,128)S(1)} %get-tuple-element.71), channel_id=1, source_target_pairs={{0,5},{1,4},{2,7},{3,6},{4,1},{5,0},{6,3},{7,2},{8,13},{9,12},{10,... | collective-permute-start | bytes 393224 | tf_op jit(solution)/shard_map/ppermute | solution.py:311
  41.8 2.4 %collective-permute-start.9 = (f32[4,2,16,256]{3,2,1,0:T(8,128)S(1)}, f32[4,2,16,256]{3,2,1,0:T(8,128)S(1)}, u32[]{:S(2)}, u32[]{:S(2)}) collective-permute-start(f32[4,2,16,256]{3,2,1,0:T(8,128)S(1)} %get-tuple-element.73), channel_id=1, source_target_pairs={{0,7},{1,6},{2,1},{3,0},{4,3},{5,2},{6,5},{7,4},{8,15},{9,14},{10,... | collective-permute-start | bytes 393224 | tf_op jit(solution)/shard_map/ppermute | solution.py:311
  44.2 1.0 collective-permute-start.27
  45.2 3.2 %collective-permute-start.28 = (f32[8,2,16,256]{3,2,1,0:T(8,128)S(1)}, f32[8,2,16,256]{3,2,1,0:T(8,128)S(1)}, u32[]{:S(2)}, u32[]{:S(2)}) collective-permute-start(f32[8,2,16,256]{3,2,1,0:T(8,128)S(1)} %get-tuple-element.97), channel_id=1, source_target_pairs={{0,16},{1,17},{2,18},{3,19},{4,20},{5,21},{6,22},{7,23},{8,24},{9,... | collective-permute-start | bytes 786440 | tf_op jit(solution)/shard_map/ppermute | solution.py:299
  48.5 3.1 %collective-permute-start.29 = (f32[8,2,16,256]{3,2,1,0:T(8,128)S(1)}, f32[8,2,16,256]{3,2,1,0:T(8,128)S(1)}, u32[]{:S(2)}, u32[]{:S(2)}) collective-permute-start(f32[8,2,16,256]{3,2,1,0:T(8,128)S(1)} %get-tuple-element.98), channel_id=1, source_target_pairs={{0,24},{1,25},{2,26},{3,27},{4,28},{5,29},{6,30},{7,31},{8,0},{9,1... | collective-permute-start | bytes 786440 | tf_op jit(solution)/shard_map/ppermute | solution.py:299
  51.6 1.3 collective-permute-done.9.refs_7_
  52.9 3.7 %shard_map.106 = (f32[8,2,16,256]{3,2,1,0:T(8,128)S(1)}, f32[8,2,16,256]{3,2,1,0:T(8,128)S(1)}, f32[8,2,16,256]{3,2,1,0:T(8,128)S(1)}, f32[8,2,16,256]{3,2,1,0:T(8,128)S(1)}) custom-call(f32[32]{0:T(128)S(1)} %copy-done.7, f32[32]{0:T(128)S(1)} %copy-done.8, f32[32]{0:T(128)S(1)} %copy-done.9, bf16[8,256,256]{2,1,0:T(8,128)(2,1)S(1)} %copy-done.10, ...), custom_call_target="tpu_custom_call" | custom-call | flops 1610612736 | bytes 4198784 | tf_op jit(solution)/shard_map/pallas_call | solution.py:271
  56.6 0.8 collective-permute-start.10
  57.4 3.2 %collective-permute-start.11 = (f32[8,2,16,256]{3,2,1,0:T(8,128)S(1)}, f32[8,2,16,256]{3,2,1,0:T(8,128)S(1)}, u32[]{:S(2)}, u32[]{:S(2)}) collective-permute-start(f32[8,2,16,256]{3,2,1,0:T(8,128)S(1)} %get-tuple-element.76), channel_id=1, source_target_pairs={{0,16},{1,17},{2,18},{3,19},{4,20},{5,21},{6,22},{7,23},{8,24},{9,... | collective-permute-start | bytes 786440 | tf_op jit(solution)/shard_map/ppermute | solution.py:299
  60.6 1.5 collective-permute-done.27.refs_1_
  62.2 1.5 collective-permute-start.12
  63.7 6.2 %collective-permute-done.29.refs_3_ = f32[8,2,16,256]{3,2,1,0:T(8,128)S(1)} collective-permute-done((f32[8,2,16,256]{3,2,1,0:T(8,128)S(1)}, f32[8,2,16,256]{3,2,1,0:T(8,128)S(1)}, u32[]{:S(2)}, u32[]{:S(2)}) %collective-permute-start.29) | collective-permute-done | bytes 262176 | tf_op jit(solution)/shard_map/ppermute | solution.py:299
  69.8 3.7 %shard_map.110 = (f32[4,2,16,256]{3,2,1,0:T(8,128)S(1)}, f32[4,2,16,256]{3,2,1,0:T(8,128)S(1)}, f32[4,2,16,256]{3,2,1,0:T(8,128)S(1)}, f32[4,2,16,256]{3,2,1,0:T...) custom-call(f32[32]{0:T(128)S(1)} %copy-done.7, ...), custom_call_target="tpu_custom_call" | custom-call | flops 1610612736 | bytes 4198784 | tf_op jit(solution)/shard_map/pallas_call | solution.py:271
  73.7 1.2 collective-permute-done.30.refs_1_
  74.9 2.0 %collective-permute-start.32 = (f32[4,2,16,256]{3,2,1,0:T(8,128)S(1)}, f32[4,2,16,256]{3,2,1,0:T(8,128)S(1)}, u32[]{:S(2)}, u32[]{:S(2)}) collective-permute-start(f32[4,2,16,256]{3,2,1,0:T(8,128)S(1)} %get-tuple-element.102), channel_id=1, source_target_pairs={{0,3},{1,2},{2,5},{3,4},{4,7},{5,6},{6,1},{7,0},{8,11},{9,10},{10,... | collective-permute-start | bytes 393224 | tf_op jit(solution)/shard_map/ppermute | solution.py:311
  77.0 23.0 %collective-permute-done.31.refs_2_ = f32[4,2,16,256]{3,2,1,0:T(8,128)S(1)} collective-permute-done((f32[4,2,16,256]{3,2,1,0:T(8,128)S(1)}, f32[4,2,16,256]{3,2,1,0:T(8,128)S(1)}, u32[]{:S(2)}, u32[]{:S(2)}) %collective-permute-start.31) | collective-permute-done | bytes 131104 | tf_op jit(solution)/shard_map/ppermute | solution.py:311
  100.0 1.6 collective-permute-start.33
  101.6 0.8 collective-permute-start.34
  102.5 2.7 %collective-permute-start.35 = (f32[4,2,16,256]{3,2,1,0:T(8,128)S(1)}, f32[4,2,16,256]{3,2,1,0:T(8,128)S(1)}, u32[]{:S(2)}, u32[]{:S(2)}) collective-permute-start(f32[4,2,16,256]{3,2,1,0:T(8,128)S(1)} %get-tuple-element.105), channel_id=1, source_target_pairs={{0,6},{1,7},{2,0},{3,1},{4,2},{5,3},{6,4},{7,5},{8,14},{9,15},{10,... | collective-permute-start | bytes 393224 | tf_op jit(solution)/shard_map/ppermute | solution.py:311
  105.1 1.5 collective-permute-start.36
  106.9 1.6 collective-permute-start.14
  108.5 0.5 collective-permute-done.34.refs_5_
  109.0 0.5 collective-permute-start.15
  109.6 2.6 %collective-permute-done.35.refs_6_ = f32[4,2,16,256]{3,2,1,0:T(8,128)S(1)} collective-permute-done((f32[4,2,16,256]{3,2,1,0:T(8,128)S(1)}, f32[4,2,16,256]{3,2,1,0:T(8,128)S(1)}, u32[]{:S(2)}, u32[]{:S(2)}) %collective-permute-start.35) | collective-permute-done | bytes 131104 | tf_op jit(solution)/shard_map/ppermute | solution.py:311
  112.1 1.5 collective-permute-start.16
  113.6 1.3 collective-permute-done.36.refs_7_
  114.9 1.3 collective-permute-start.17
  116.2 3.0 %collective-permute-start.37 = (f32[8,2,16,256]{3,2,1,0:T(8,128)S(1)}, f32[8,2,16,256]{3,2,1,0:T(8,128)S(1)}, u32[]{:S(2)}, u32[]{:S(2)}) collective-permute-start(f32[8,2,16,256]{3,2,1,0:T(8,128)S(1)} %get-tuple-element.108), channel_id=1, source_target_pairs={{0,8},{1,9},{2,10},{3,11},{4,12},{5,13},{6,14},{7,15},{8,16},{9,17... | collective-permute-start | bytes 786440 | tf_op jit(solution)/shard_map/ppermute | solution.py:299
  119.2 3.7 %collective-permute-start.39 = (f32[8,2,16,256]{3,2,1,0:T(8,128)S(1)}, f32[8,2,16,256]{3,2,1,0:T(8,128)S(1)}, u32[]{:S(2)}, u32[]{:S(2)}) collective-permute-start(f32[8,2,16,256]{3,2,1,0:T(8,128)S(1)} %get-tuple-element.110), channel_id=1, source_target_pairs={{0,24},{1,25},{2,26},{3,27},{4,28},{5,29},{6,30},{7,31},{8,0},{9,1... | collective-permute-start | bytes 786440 | tf_op jit(solution)/shard_map/ppermute | solution.py:299
  122.9 1.5 collective-permute-start.18
  124.4 0.8 collective-permute-start.19
  125.2 3.9 %collective-permute-done.18.refs_6_ = f32[4,2,16,256]{3,2,1,0:T(8,128)S(1)} collective-permute-done((f32[4,2,16,256]{3,2,1,0:T(8,128)S(1)}, f32[4,2,16,256]{3,2,1,0:T(8,128)S(1)}, u32[]{:S(2)}, u32[]{:S(2)}) %collective-permute-start.18) | collective-permute-done | bytes 131104 | tf_op jit(solution)/shard_map/ppermute | solution.py:311
  129.1 1.4 collective-permute-done.19.refs_7_
  130.6 3.5 %collective-permute-start.40 = (f32[4,16,256]{2,1,0:T(8,128)S(1)}, f32[4,16,256]{2,1,0:T(8,128)S(1)}, u32[]{:S(2)}, u32[]{:S(2)}) collective-permute-start(f32[4,16,256]{2,1,0:T(8,128)S(1)} %get-tuple-element.118), channel_id=1, source_target_pairs={{0,32},{32,64},{64,96},{96,128},{128,160},{160,192},{192,224},{1,3... | collective-permute-start | bytes 196616 | tf_op jit(solution)/shard_map/ppermute | solution.py:315
  134.1 4.6 %collective-permute-start.41 = (f32[4,16,256]{2,1,0:T(8,128)S(1)}, f32[4,16,256]{2,1,0:T(8,128)S(1)}, u32[]{:S(2)}, u32[]{:S(2)}) collective-permute-start(f32[4,16,256]{2,1,0:T(8,128)S(1)} %get-tuple-element.119), channel_id=1, source_target_pairs={{32,0},{64,32},{96,64},{128,96},{160,128},{192,160},{224,192},{33,... | collective-permute-start | bytes 196616 | tf_op jit(solution)/shard_map/ppermute | solution.py:315
  138.7 5.3 %collective-permute-done.37.refs_1_ = f32[8,2,16,256]{3,2,1,0:T(8,128)S(1)} collective-permute-done((f32[8,2,16,256]{3,2,1,0:T(8,128)S(1)}, f32[8,2,16,256]{3,2,1,0:T(8,128)S(1)}, u32[]{:S(2)}, u32[]{:S(2)}) %collective-permute-start.37) | collective-permute-done | bytes 262176 | tf_op jit(solution)/shard_map/ppermute | solution.py:299
  144.1 3.5 %collective-permute-start.42 = (f32[2,16,256]{2,1,0:T(8,128)S(1)}, f32[2,16,256]{2,1,0:T(8,128)S(1)}, u32[]{:S(2)}, u32[]{:S(2)}) collective-permute-start(f32[2,16,256]{2,1,0:T(8,128)S(1)} %get-tuple-element.120), channel_id=1, source_target_pairs={{0,32},{32,64},{64,96},{96,128},{128,160},{160,192},{192,224},{1,3... | collective-permute-start | bytes 98312 | tf_op jit(solution)/shard_map/ppermute | solution.py:315
  147.6 6.2 %collective-permute-start.43 = (f32[2,16,256]{2,1,0:T(8,128)S(1)}, f32[2,16,256]{2,1,0:T(8,128)S(1)}, u32[]{:S(2)}, u32[]{:S(2)}) collective-permute-start(f32[2,16,256]{2,1,0:T(8,128)S(1)} %get-tuple-element.121), channel_id=1, source_target_pairs={{32,0},{64,32},{96,64},{128,96},{160,128},{192,160},{224,192},{33,... | collective-permute-start | bytes 98312 | tf_op jit(solution)/shard_map/ppermute | solution.py:315
  153.8 2.5 %shard_map.113 = (f32[32,16,512]{2,1,0:T(8,128)}, f32[32,16,512]{2,1,0:T(8,128)}, f32[1,16,512]{2,1,0:T(8,128)S(1)}, f32[1,16,512]{2,1,0:T(8,128)S(1)}, f32[1,16...) custom-call(f32[32,2,16,256]{3,2,1,0:T(8,128)S(1)} %get-tuple-element.86.even_ref, ...), custom_call_target="tpu_custom_call" | custom-call | bytes 5373952 | tf_op jit(solution)/shard_map/pallas_call | solution.py:271
  156.3 0.6 copy-done.3
  156.9 0.6 copy-done.4
  157.5 0.6 copy-done.5
  158.1 0.6 copy-done.6
  158.8 0.5 copy-done.15
  159.4 1.8 %outer.1 = (f32[32,16,512]{2,1,0:T(8,128)}, f32[32,16,512]{2,1,0:T(8,128)}) custom-call(f32[32,16,512]{2,1,0:T(8,128)} %get-tuple-element.112.t_ref, f32[32,16,512]{2,1,0:T(8,128)} %get-tuple-element.113.s_ref, f32[1,16,512]{2,1,0:T(8,128)} %copy-done.3, f32[1,16,512]{2,1,0:T(8,128)} %copy-done.4, ...), custom_call_target="tpu_custom_call", output_to_operand_aliasing={{0}: (0, {}), {1}: (1, {})} | custom-call | tf_op jit(solution)/shard_map/outer/pallas_call | solution.py:359
  (69 shorter events, 1.2 us)
Async XLA Ops:
  0.6 1.2 copy-start.1
  1.9 1.2 copy-start.2
  3.2 24.7 %collective-permute-start = (f32[8,2,16,256]{3,2,1,0:T(8,128)S(1)}, f32[8,2,16,256]{3,2,1,0:T(8,128)S(1)}, u32[]{:S(2)}, u32[]{:S(2)}) collective-permute-start(f32[8,2,16,256]{3,2,1,0:T(8,128)S(1)} %get-tuple-element.63), channel_id=1, source_target_pairs={{0,8},{1,9},{2,10},{3,11},{4,12},{5,13},{6,14},{7,15},{8,16},{9,17... | collective-permute-start | bytes 786440 | tf_op jit(solution)/shard_map/ppermute | solution.py:299
  6.6 22.0 %collective-permute-start.1 = (f32[8,2,16,256]{3,2,1,0:T(8,128)S(1)}, f32[8,2,16,256]{3,2,1,0:T(8,128)S(1)}, u32[]{:S(2)}, u32[]{:S(2)}) collective-permute-start(f32[8,2,16,256]{3,2,1,0:T(8,128)S(1)} %get-tuple-element.64), channel_id=1, source_target_pairs={{0,16},{1,17},{2,18},{3,19},{4,20},{5,21},{6,22},{7,23},{8,24},{9,... | collective-permute-start | bytes 786440 | tf_op jit(solution)/shard_map/ppermute | solution.py:299
  11.1 19.0 %collective-permute-start.2 = (f32[8,2,16,256]{3,2,1,0:T(8,128)S(1)}, f32[8,2,16,256]{3,2,1,0:T(8,128)S(1)}, u32[]{:S(2)}, u32[]{:S(2)}) collective-permute-start(f32[8,2,16,256]{3,2,1,0:T(8,128)S(1)} %get-tuple-element.65), channel_id=1, source_target_pairs={{0,24},{1,25},{2,26},{3,27},{4,28},{5,29},{6,30},{7,31},{8,0},{9,1... | collective-permute-start | bytes 786440 | tf_op jit(solution)/shard_map/ppermute | solution.py:299
  13.7 1.5 collective-permute-start.20
  13.7 6.4 %collective-permute-start.21 = (f32[4,2,16,256]{3,2,1,0:T(8,128)S(1)}, f32[4,2,16,256]{3,2,1,0:T(8,128)S(1)}, u32[]{:S(2)}, u32[]{:S(2)}) collective-permute-start(f32[4,2,16,256]{3,2,1,0:T(8,128)S(1)} %get-tuple-element.89), channel_id=1, source_target_pairs={{0,2},{1,3},{2,4},{3,5},{4,6},{5,7},{6,0},{7,1},{8,10},{9,11},{10,... | collective-permute-start | bytes 393224 | tf_op jit(solution)/shard_map/ppermute | solution.py:311
  15.2 16.9 %collective-permute-start.22 = (f32[4,2,16,256]{3,2,1,0:T(8,128)S(1)}, f32[4,2,16,256]{3,2,1,0:T(8,128)S(1)}, u32[]{:S(2)}, u32[]{:S(2)}) collective-permute-start(f32[4,2,16,256]{3,2,1,0:T(8,128)S(1)} %get-tuple-element.90), channel_id=1, source_target_pairs={{0,3},{1,2},{2,5},{3,4},{4,7},{5,6},{6,1},{7,0},{8,11},{9,10},{10,... | collective-permute-start | bytes 393224 | tf_op jit(solution)/shard_map/ppermute | solution.py:311
  20.1 12.1 %collective-permute-start.23 = (f32[4,2,16,256]{3,2,1,0:T(8,128)S(1)}, f32[4,2,16,256]{3,2,1,0:T(8,128)S(1)}, u32[]{:S(2)}, u32[]{:S(2)}) collective-permute-start(f32[4,2,16,256]{3,2,1,0:T(8,128)S(1)} %get-tuple-element.91), channel_id=1, source_target_pairs={{0,4},{1,5},{2,6},{3,7},{4,0},{5,1},{6,2},{7,3},{8,12},{9,13},{10,... | collective-permute-start | bytes 393224 | tf_op jit(solution)/shard_map/ppermute | solution.py:311
  27.9 7.3 %collective-permute-start.24 = (f32[4,2,16,256]{3,2,1,0:T(8,128)S(1)}, f32[4,2,16,256]{3,2,1,0:T(8,128)S(1)}, u32[]{:S(2)}, u32[]{:S(2)}) collective-permute-start(f32[4,2,16,256]{3,2,1,0:T(8,128)S(1)} %get-tuple-element.92), channel_id=1, source_target_pairs={{0,5},{1,4},{2,7},{3,6},{4,1},{5,0},{6,3},{7,2},{8,13},{9,12},{10,... | collective-permute-start | bytes 393224 | tf_op jit(solution)/shard_map/ppermute | solution.py:311
  28.6 8.5 %collective-permute-start.25 = (f32[4,2,16,256]{3,2,1,0:T(8,128)S(1)}, f32[4,2,16,256]{3,2,1,0:T(8,128)S(1)}, u32[]{:S(2)}, u32[]{:S(2)}) collective-permute-start(f32[4,2,16,256]{3,2,1,0:T(8,128)S(1)} %get-tuple-element.93), channel_id=1, source_target_pairs={{0,6},{1,7},{2,0},{3,1},{4,2},{5,3},{6,4},{7,5},{8,14},{9,15},{10,... | collective-permute-start | bytes 393224 | tf_op jit(solution)/shard_map/ppermute | solution.py:311
  30.1 9.9 %collective-permute-start.26 = (f32[4,2,16,256]{3,2,1,0:T(8,128)S(1)}, f32[4,2,16,256]{3,2,1,0:T(8,128)S(1)}, u32[]{:S(2)}, u32[]{:S(2)}) collective-permute-start(f32[4,2,16,256]{3,2,1,0:T(8,128)S(1)} %get-tuple-element.94), channel_id=1, source_target_pairs={{0,7},{1,6},{2,1},{3,0},{4,3},{5,2},{6,5},{7,4},{8,15},{9,14},{10,... | collective-permute-start | bytes 393224 | tf_op jit(solution)/shard_map/ppermute | solution.py:311
  32.0 20.8 %copy-start.10 = (bf16[8,256,256]{2,1,0:T(8,128)(2,1)S(1)}, bf16[8,256,256]{2,1,0:T(8,128)(2,1)}, u32[]{:S(2)}) copy-start(bf16[8,256,256]{2,1,0:T(8,128)(2,1)} %constant.6.clone.tab_ref) | copy-start | bytes 3145732
  32.1 9.6 %collective-permute-start.3 = (f32[4,2,16,256]{3,2,1,0:T(8,128)S(1)}, f32[4,2,16,256]{3,2,1,0:T(8,128)S(1)}, u32[]{:S(2)}, u32[]{:S(2)}) collective-permute-start(f32[4,2,16,256]{3,2,1,0:T(8,128)S(1)} %get-tuple-element.67), channel_id=1, source_target_pairs={{0,1},{1,0},{2,3},{3,2},{4,5},{5,4},{6,7},{7,6},{8,9},{9,8},{10,11... | collective-permute-start | bytes 393224 | tf_op jit(solution)/shard_map/ppermute | solution.py:311
  32.2 9.5 %collective-permute-start.4 = (f32[4,2,16,256]{3,2,1,0:T(8,128)S(1)}, f32[4,2,16,256]{3,2,1,0:T(8,128)S(1)}, u32[]{:S(2)}, u32[]{:S(2)}) collective-permute-start(f32[4,2,16,256]{3,2,1,0:T(8,128)S(1)} %get-tuple-element.68), channel_id=1, source_target_pairs={{0,2},{1,3},{2,4},{3,5},{4,6},{5,7},{6,0},{7,1},{8,10},{9,11},{10,... | collective-permute-start | bytes 393224 | tf_op jit(solution)/shard_map/ppermute | solution.py:311
  35.2 9.0 %collective-permute-start.5 = (f32[4,2,16,256]{3,2,1,0:T(8,128)S(1)}, f32[4,2,16,256]{3,2,1,0:T(8,128)S(1)}, u32[]{:S(2)}, u32[]{:S(2)}) collective-permute-start(f32[4,2,16,256]{3,2,1,0:T(8,128)S(1)} %get-tuple-element.69), channel_id=1, source_target_pairs={{0,3},{1,2},{2,5},{3,4},{4,7},{5,6},{6,1},{7,0},{8,11},{9,10},{10,... | collective-permute-start | bytes 393224 | tf_op jit(solution)/shard_map/ppermute | solution.py:311
  37.1 8.1 %collective-permute-start.6 = (f32[4,2,16,256]{3,2,1,0:T(8,128)S(1)}, f32[4,2,16,256]{3,2,1,0:T(8,128)S(1)}, u32[]{:S(2)}, u32[]{:S(2)}) collective-permute-start(f32[4,2,16,256]{3,2,1,0:T(8,128)S(1)} %get-tuple-element.70), channel_id=1, source_target_pairs={{0,4},{1,5},{2,6},{3,7},{4,0},{5,1},{6,2},{7,3},{8,12},{9,13},{10,... | collective-permute-start | bytes 393224 | tf_op jit(solution)/shard_map/ppermute | solution.py:311
  40.0 8.5 %collective-permute-start.7 = (f32[4,2,16,256]{3,2,1,0:T(8,128)S(1)}, f32[4,2,16,256]{3,2,1,0:T(8,128)S(1)}, u32[]{:S(2)}, u32[]{:S(2)}) collective-permute-start(f32[4,2,16,256]{3,2,1,0:T(8,128)S(1)} %get-tuple-element.71), channel_id=1, source_target_pairs={{0,5},{1,4},{2,7},{3,6},{4,1},{5,0},{6,3},{7,2},{8,13},{9,12},{10,... | collective-permute-start | bytes 393224 | tf_op jit(solution)/shard_map/ppermute | solution.py:311
  41.8 9.8 %collective-permute-start.8 = (f32[4,2,16,256]{3,2,1,0:T(8,128)S(1)}, f32[4,2,16,256]{3,2,1,0:T(8,128)S(1)}, u32[]{:S(2)}, u32[]{:S(2)}) collective-permute-start(f32[4,2,16,256]{3,2,1,0:T(8,128)S(1)} %get-tuple-element.72), channel_id=1, source_target_pairs={{0,6},{1,7},{2,0},{3,1},{4,2},{5,3},{6,4},{7,5},{8,14},{9,15},{10,... | collective-permute-start | bytes 393224 | tf_op jit(solution)/shard_map/ppermute | solution.py:311
  41.8 11.1 %collective-permute-start.9 = (f32[4,2,16,256]{3,2,1,0:T(8,128)S(1)}, f32[4,2,16,256]{3,2,1,0:T(8,128)S(1)}, u32[]{:S(2)}, u32[]{:S(2)}) collective-permute-start(f32[4,2,16,256]{3,2,1,0:T(8,128)S(1)} %get-tuple-element.73), channel_id=1, source_target_pairs={{0,7},{1,6},{2,1},{3,0},{4,3},{5,2},{6,5},{7,4},{8,15},{9,14},{10,... | collective-permute-start | bytes 393224 | tf_op jit(solution)/shard_map/ppermute | solution.py:311
  44.1 8.7 %copy-start.11 = (f32[256,2]{1,0:T(8,128)S(1)}, f32[256,2]{1,0:T(8,128)}, u32[]{:S(2)}) copy-start(f32[256,2]{1,0:T(8,128)} %constant.7.clone.sq_ref) | copy-start | bytes 6148
  44.2 17.9 %collective-permute-start.27 = (f32[8,2,16,256]{3,2,1,0:T(8,128)S(1)}, f32[8,2,16,256]{3,2,1,0:T(8,128)S(1)}, u32[]{:S(2)}, u32[]{:S(2)}) collective-permute-start(f32[8,2,16,256]{3,2,1,0:T(8,128)S(1)} %get-tuple-element.96), channel_id=1, source_target_pairs={{0,8},{1,9},{2,10},{3,11},{4,12},{5,13},{6,14},{7,15},{8,16},{9,17... | collective-permute-start | bytes 786440 | tf_op jit(solution)/shard_map/ppermute | solution.py:299
  45.2 7.6 %copy-start.12 = (f32[2,256]{1,0:T(2,128)S(1)}, f32[2,256]{1,0:T(2,128)}, u32[]{:S(2)}) copy-start(f32[2,256]{1,0:T(2,128)} %constant.8.clone.sqt_ref) | copy-start | bytes 6148
  45.2 18.5 %collective-permute-start.28 = (f32[8,2,16,256]{3,2,1,0:T(8,128)S(1)}, f32[8,2,16,256]{3,2,1,0:T(8,128)S(1)}, u32[]{:S(2)}, u32[]{:S(2)}) collective-permute-start(f32[8,2,16,256]{3,2,1,0:T(8,128)S(1)} %get-tuple-element.97), channel_id=1, source_target_pairs={{0,16},{1,17},{2,18},{3,19},{4,20},{5,21},{6,22},{7,23},{8,24},{9,... | collective-permute-start | bytes 786440 | tf_op jit(solution)/shard_map/ppermute | solution.py:299
  48.5 4.4 %copy-start.7 = (f32[32]{0:T(128)S(1)}, f32[32]{0:T(128)}, u32[]{:S(2)}) copy-start(f32[32]{0:T(128)} %rt_ref.3) | copy-start | bytes 388
  48.5 4.4 %copy-start.8 = (f32[32]{0:T(128)S(1)}, f32[32]{0:T(128)}, u32[]{:S(2)}) copy-start(f32[32]{0:T(128)} %rs_ref.3) | copy-start | bytes 388
  48.5 4.4 %copy-start.9 = (f32[32]{0:T(128)S(1)}, f32[32]{0:T(128)}, u32[]{:S(2)}) copy-start(f32[32]{0:T(128)} %rc_ref.3) | copy-start | bytes 388
  48.5 21.4 %collective-permute-start.29 = (f32[8,2,16,256]{3,2,1,0:T(8,128)S(1)}, f32[8,2,16,256]{3,2,1,0:T(8,128)S(1)}, u32[]{:S(2)}, u32[]{:S(2)}) collective-permute-start(f32[8,2,16,256]{3,2,1,0:T(8,128)S(1)} %get-tuple-element.98), channel_id=1, source_target_pairs={{0,24},{1,25},{2,26},{3,27},{4,28},{5,29},{6,30},{7,31},{8,0},{9,1... | collective-permute-start | bytes 786440 | tf_op jit(solution)/shard_map/ppermute | solution.py:299
  56.6 45.1 %collective-permute-start.10 = (f32[8,2,16,256]{3,2,1,0:T(8,128)S(1)}, f32[8,2,16,256]{3,2,1,0:T(8,128)S(1)}, u32[]{:S(2)}, u32[]{:S(2)}) collective-permute-start(f32[8,2,16,256]{3,2,1,0:T(8,128)S(1)} %get-tuple-element.75), channel_id=1, source_target_pairs={{0,8},{1,9},{2,10},{3,11},{4,12},{5,13},{6,14},{7,15},{8,16},{9,17... | collective-permute-start | bytes 786440 | tf_op jit(solution)/shard_map/ppermute | solution.py:299
  57.4 45.1 %collective-permute-start.11 = (f32[8,2,16,256]{3,2,1,0:T(8,128)S(1)}, f32[8,2,16,256]{3,2,1,0:T(8,128)S(1)}, u32[]{:S(2)}, u32[]{:S(2)}) collective-permute-start(f32[8,2,16,256]{3,2,1,0:T(8,128)S(1)} %get-tuple-element.76), channel_id=1, source_target_pairs={{0,16},{1,17},{2,18},{3,19},{4,20},{5,21},{6,22},{7,23},{8,24},{9,... | collective-permute-start | bytes 786440 | tf_op jit(solution)/shard_map/ppermute | solution.py:299
  62.2 43.0 %collective-permute-start.12 = (f32[8,2,16,256]{3,2,1,0:T(8,128)S(1)}, f32[8,2,16,256]{3,2,1,0:T(8,128)S(1)}, u32[]{:S(2)}, u32[]{:S(2)}) collective-permute-start(f32[8,2,16,256]{3,2,1,0:T(8,128)S(1)} %get-tuple-element.77), channel_id=1, source_target_pairs={{0,24},{1,25},{2,26},{3,27},{4,28},{5,29},{6,30},{7,31},{8,0},{9,1... | collective-permute-start | bytes 786440 | tf_op jit(solution)/shard_map/ppermute | solution.py:299
  73.5 1.4 collective-permute-start.30
  73.6 26.4 %collective-permute-start.31 = (f32[4,2,16,256]{3,2,1,0:T(8,128)S(1)}, f32[4,2,16,256]{3,2,1,0:T(8,128)S(1)}, u32[]{:S(2)}, u32[]{:S(2)}) collective-permute-start(f32[4,2,16,256]{3,2,1,0:T(8,128)S(1)} %get-tuple-element.101), channel_id=1, source_target_pairs={{0,2},{1,3},{2,4},{3,5},{4,6},{5,7},{6,0},{7,1},{8,10},{9,11},{10,... | collective-permute-start | bytes 393224 | tf_op jit(solution)/shard_map/ppermute | solution.py:311
  74.9 31.7 %collective-permute-start.32 = (f32[4,2,16,256]{3,2,1,0:T(8,128)S(1)}, f32[4,2,16,256]{3,2,1,0:T(8,128)S(1)}, u32[]{:S(2)}, u32[]{:S(2)}) collective-permute-start(f32[4,2,16,256]{3,2,1,0:T(8,128)S(1)} %get-tuple-element.102), channel_id=1, source_target_pairs={{0,3},{1,2},{2,5},{3,4},{4,7},{5,6},{6,1},{7,0},{8,11},{9,10},{10,... | collective-permute-start | bytes 393224 | tf_op jit(solution)/shard_map/ppermute | solution.py:311
  100.0 6.9 %collective-permute-start.33 = (f32[4,2,16,256]{3,2,1,0:T(8,128)S(1)}, f32[4,2,16,256]{3,2,1,0:T(8,128)S(1)}, u32[]{:S(2)}, u32[]{:S(2)}) collective-permute-start(f32[4,2,16,256]{3,2,1,0:T(8,128)S(1)} %get-tuple-element.103), channel_id=1, source_target_pairs={{0,4},{1,5},{2,6},{3,7},{4,0},{5,1},{6,2},{7,3},{8,12},{9,13},{10,... | collective-permute-start | bytes 393224 | tf_op jit(solution)/shard_map/ppermute | solution.py:311
  101.6 7.4 %collective-permute-start.34 = (f32[4,2,16,256]{3,2,1,0:T(8,128)S(1)}, f32[4,2,16,256]{3,2,1,0:T(8,128)S(1)}, u32[]{:S(2)}, u32[]{:S(2)}) collective-permute-start(f32[4,2,16,256]{3,2,1,0:T(8,128)S(1)} %get-tuple-element.104), channel_id=1, source_target_pairs={{0,5},{1,4},{2,7},{3,6},{4,1},{5,0},{6,3},{7,2},{8,13},{9,12},{10,... | collective-permute-start | bytes 393224 | tf_op jit(solution)/shard_map/ppermute | solution.py:311
  102.5 9.7 %collective-permute-start.35 = (f32[4,2,16,256]{3,2,1,0:T(8,128)S(1)}, f32[4,2,16,256]{3,2,1,0:T(8,128)S(1)}, u32[]{:S(2)}, u32[]{:S(2)}) collective-permute-start(f32[4,2,16,256]{3,2,1,0:T(8,128)S(1)} %get-tuple-element.105), channel_id=1, source_target_pairs={{0,6},{1,7},{2,0},{3,1},{4,2},{5,3},{6,4},{7,5},{8,14},{9,15},{10,... | collective-permute-start | bytes 393224 | tf_op jit(solution)/shard_map/ppermute | solution.py:311
  105.1 9.8 %collective-permute-start.36 = (f32[4,2,16,256]{3,2,1,0:T(8,128)S(1)}, f32[4,2,16,256]{3,2,1,0:T(8,128)S(1)}, u32[]{:S(2)}, u32[]{:S(2)}) collective-permute-start(f32[4,2,16,256]{3,2,1,0:T(8,128)S(1)} %get-tuple-element.106), channel_id=1, source_target_pairs={{0,7},{1,6},{2,1},{3,0},{4,3},{5,2},{6,5},{7,4},{8,15},{9,14},{10,... | collective-permute-start | bytes 393224 | tf_op jit(solution)/shard_map/ppermute | solution.py:311
  106.6 23.9 %copy-start = (f32[32,16,512]{2,1,0:T(8,128)S(1)}, f32[32,16,512]{2,1,0:T(8,128)}, u32[]{:S(2)}) copy-start(f32[32,16,512]{2,1,0:T(8,128)} %wl_ref.1) | copy-start | bytes 3145732
  106.7 9.5 %collective-permute-start.13 = (f32[4,2,16,256]{3,2,1,0:T(8,128)S(1)}, f32[4,2,16,256]{3,2,1,0:T(8,128)S(1)}, u32[]{:S(2)}, u32[]{:S(2)}) collective-permute-start(f32[4,2,16,256]{3,2,1,0:T(8,128)S(1)} %get-tuple-element.79), channel_id=1, source_target_pairs={{0,1},{1,0},{2,3},{3,2},{4,5},{5,4},{6,7},{7,6},{8,9},{9,8},{10,11... | collective-permute-start | bytes 393224 | tf_op jit(solution)/shard_map/ppermute | solution.py:311
  106.9 12.3 %collective-permute-start.14 = (f32[4,2,16,256]{3,2,1,0:T(8,128)S(1)}, f32[4,2,16,256]{3,2,1,0:T(8,128)S(1)}, u32[]{:S(2)}, u32[]{:S(2)}) collective-permute-start(f32[4,2,16,256]{3,2,1,0:T(8,128)S(1)} %get-tuple-element.80), channel_id=1, source_target_pairs={{0,2},{1,3},{2,4},{3,5},{4,6},{5,7},{6,0},{7,1},{8,10},{9,11},{10,... | collective-permute-start | bytes 393224 | tf_op jit(solution)/shard_map/ppermute | solution.py:311
  109.0 10.2 %collective-permute-start.15 = (f32[4,2,16,256]{3,2,1,0:T(8,128)S(1)}, f32[4,2,16,256]{3,2,1,0:T(8,128)S(1)}, u32[]{:S(2)}, u32[]{:S(2)}) collective-permute-start(f32[4,2,16,256]{3,2,1,0:T(8,128)S(1)} %get-tuple-element.81), channel_id=1, source_target_pairs={{0,3},{1,2},{2,5},{3,4},{4,7},{5,6},{6,1},{7,0},{8,11},{9,10},{10,... | collective-permute-start | bytes 393224 | tf_op jit(solution)/shard_map/ppermute | solution.py:311
  112.1 10.8 %collective-permute-start.16 = (f32[4,2,16,256]{3,2,1,0:T(8,128)S(1)}, f32[4,2,16,256]{3,2,1,0:T(8,128)S(1)}, u32[]{:S(2)}, u32[]{:S(2)}) collective-permute-start(f32[4,2,16,256]{3,2,1,0:T(8,128)S(1)} %get-tuple-element.82), channel_id=1, source_target_pairs={{0,4},{1,5},{2,6},{3,7},{4,0},{5,1},{6,2},{7,3},{8,12},{9,13},{10,... | collective-permute-start | bytes 393224 | tf_op jit(solution)/shard_map/ppermute | solution.py:311
  114.9 9.5 %collective-permute-start.17 = (f32[4,2,16,256]{3,2,1,0:T(8,128)S(1)}, f32[4,2,16,256]{3,2,1,0:T(8,128)S(1)}, u32[]{:S(2)}, u32[]{:S(2)}) collective-permute-start(f32[4,2,16,256]{3,2,1,0:T(8,128)S(1)} %get-tuple-element.83), channel_id=1, source_target_pairs={{0,5},{1,4},{2,7},{3,6},{4,1},{5,0},{6,3},{7,2},{8,13},{9,12},{10,... | collective-permute-start | bytes 393224 | tf_op jit(solution)/shard_map/ppermute | solution.py:311
  116.2 27.7 %collective-permute-start.37 = (f32[8,2,16,256]{3,2,1,0:T(8,128)S(1)}, f32[8,2,16,256]{3,2,1,0:T(8,128)S(1)}, u32[]{:S(2)}, u32[]{:S(2)}) collective-permute-start(f32[8,2,16,256]{3,2,1,0:T(8,128)S(1)} %get-tuple-element.108), channel_id=1, source_target_pairs={{0,8},{1,9},{2,10},{3,11},{4,12},{5,13},{6,14},{7,15},{8,16},{9,17... | collective-permute-start | bytes 786440 | tf_op jit(solution)/shard_map/ppermute | solution.py:299
  119.2 24.8 %collective-permute-start.38 = (f32[8,2,16,256]{3,2,1,0:T(8,128)S(1)}, f32[8,2,16,256]{3,2,1,0:T(8,128)S(1)}, u32[]{:S(2)}, u32[]{:S(2)}) collective-permute-start(f32[8,2,16,256]{3,2,1,0:T(8,128)S(1)} %get-tuple-element.109), channel_id=1, source_target_pairs={{0,16},{1,17},{2,18},{3,19},{4,20},{5,21},{6,22},{7,23},{8,24},{9,... | collective-permute-start | bytes 786440 | tf_op jit(solution)/shard_map/ppermute | solution.py:299
  119.2 24.8 %collective-permute-start.39 = (f32[8,2,16,256]{3,2,1,0:T(8,128)S(1)}, f32[8,2,16,256]{3,2,1,0:T(8,128)S(1)}, u32[]{:S(2)}, u32[]{:S(2)}) collective-permute-start(f32[8,2,16,256]{3,2,1,0:T(8,128)S(1)} %get-tuple-element.110), channel_id=1, source_target_pairs={{0,24},{1,25},{2,26},{3,27},{4,28},{5,29},{6,30},{7,31},{8,0},{9,1... | collective-permute-start | bytes 786440 | tf_op jit(solution)/shard_map/ppermute | solution.py:299
  122.9 6.2 %collective-permute-start.18 = (f32[4,2,16,256]{3,2,1,0:T(8,128)S(1)}, f32[4,2,16,256]{3,2,1,0:T(8,128)S(1)}, u32[]{:S(2)}, u32[]{:S(2)}) collective-permute-start(f32[4,2,16,256]{3,2,1,0:T(8,128)S(1)} %get-tuple-element.84), channel_id=1, source_target_pairs={{0,6},{1,7},{2,0},{3,1},{4,2},{5,3},{6,4},{7,5},{8,14},{9,15},{10,... | collective-permute-start | bytes 393224 | tf_op jit(solution)/shard_map/ppermute | solution.py:311
  124.4 6.1 %collective-permute-start.19 = (f32[4,2,16,256]{3,2,1,0:T(8,128)S(1)}, f32[4,2,16,256]{3,2,1,0:T(8,128)S(1)}, u32[]{:S(2)}, u32[]{:S(2)}) collective-permute-start(f32[4,2,16,256]{3,2,1,0:T(8,128)S(1)} %get-tuple-element.85), channel_id=1, source_target_pairs={{0,7},{1,6},{2,1},{3,0},{4,3},{5,2},{6,5},{7,4},{8,15},{9,14},{10,... | collective-permute-start | bytes 393224 | tf_op jit(solution)/shard_map/ppermute | solution.py:311
  130.6 28.2 %collective-permute-start.40 = (f32[4,16,256]{2,1,0:T(8,128)S(1)}, f32[4,16,256]{2,1,0:T(8,128)S(1)}, u32[]{:S(2)}, u32[]{:S(2)}) collective-permute-start(f32[4,16,256]{2,1,0:T(8,128)S(1)} %get-tuple-element.118), channel_id=1, source_target_pairs={{0,32},{32,64},{64,96},{96,128},{128,160},{160,192},{192,224},{1,3... | collective-permute-start | bytes 196616 | tf_op jit(solution)/shard_map/ppermute | solution.py:315
  134.1 24.7 %collective-permute-start.41 = (f32[4,16,256]{2,1,0:T(8,128)S(1)}, f32[4,16,256]{2,1,0:T(8,128)S(1)}, u32[]{:S(2)}, u32[]{:S(2)}) collective-permute-start(f32[4,16,256]{2,1,0:T(8,128)S(1)} %get-tuple-element.119), channel_id=1, source_target_pairs={{32,0},{64,32},{96,64},{128,96},{160,128},{192,160},{224,192},{33,... | collective-permute-start | bytes 196616 | tf_op jit(solution)/shard_map/ppermute | solution.py:315
  144.1 14.6 %collective-permute-start.42 = (f32[2,16,256]{2,1,0:T(8,128)S(1)}, f32[2,16,256]{2,1,0:T(8,128)S(1)}, u32[]{:S(2)}, u32[]{:S(2)}) collective-permute-start(f32[2,16,256]{2,1,0:T(8,128)S(1)} %get-tuple-element.120), channel_id=1, source_target_pairs={{0,32},{32,64},{64,96},{96,128},{128,160},{160,192},{192,224},{1,3... | collective-permute-start | bytes 98312 | tf_op jit(solution)/shard_map/ppermute | solution.py:315
  147.6 11.2 %collective-permute-start.43 = (f32[2,16,256]{2,1,0:T(8,128)S(1)}, f32[2,16,256]{2,1,0:T(8,128)S(1)}, u32[]{:S(2)}, u32[]{:S(2)}) collective-permute-start(f32[2,16,256]{2,1,0:T(8,128)S(1)} %get-tuple-element.121), channel_id=1, source_target_pairs={{32,0},{64,32},{96,64},{128,96},{160,128},{192,160},{224,192},{33,... | collective-permute-start | bytes 98312 | tf_op jit(solution)/shard_map/ppermute | solution.py:315
  156.3 0.6 copy-start.3
  156.9 0.6 copy-start.4
  157.5 0.6 copy-start.5
  158.1 0.6 copy-start.6
  158.7 0.6 copy-start.15
  158.8 0.6 copy-start.16
  158.8 0.6 copy-start.13
  158.8 0.6 copy-start.14
